TPU v7x, 32 devices: a whole 2x2x4 slice. The times are simulated.
32 devices in a mesh: member: 8 (over z, x), cell: 4 (over y, core).
Axes of the slice: x: 2, y: 2, z: 4, core: 2. Of those that a mesh axis runs over, the one named last changes fastest.
Arguments:
- latent: bfloat16 [8, 6144, 1024], P('member', 'cell'), may hold values from -6 to 6
- w_in: bfloat16 [1024, 1024], replicated, may hold values from -0.1875 to 0.1875
- w_out: bfloat16 [1024, 96], replicated, may hold values from -0.1875 to 0.1875
- target: bfloat16 [96, 6144], P(None, 'cell'), may hold values from -6 to 6
- cell_mask: int32 [6144], P('cell'), may hold values 0 or 1
Outputs:
- grad_w_in: float32 [1024, 1024], P(('member', 'cell'))
- grad_w_out: float32 [1024, 96], P(('member', 'cell'))
All inputs are finite; a program needn't handle non-finite values. No bound on the sum of `cell_mask` on one device may be relied on, other than what follows from the above.
Results may differ from a plain program's by a relative error of at most 0.0055.
Values may be sent and summed in bfloat16 or wider, within the bound.
A program may use at most 64 MiB of HBM per device.

v0:
```python
import functools

import jax
import jax.numpy as jnp
from jax import lax
from jax.experimental import pallas as pl
from jax.experimental.pallas import tpu as pltpu
from jax.sharding import PartitionSpec as P

MESH = pl.DeviceIdType.MESH
BF = jnp.bfloat16
F32 = jnp.float32


def sigmoid(v):
    return 0.5 * jnp.tanh(0.5 * v) + 0.5


def smooth(d):
    return d * lax.rsqrt(1.0 + d * d)


def mm(a, b):
    return jnp.dot(a, b, preferred_element_type=F32)


def body(
    M, CN,
    lat_hbm, w_in_hbm, w_out, target, mask, out_in, out_out,
    lat, w_in, slope, hid, gp, lat_t, hid_t, tgt_t, wgt_t,
    fsend, frecv, gsend, gf,
    acc_f, acc_b, r1, k2, s2, r2, s3, r3, k3,
    sem_in, sem_fs, sem_fr, sem_gs, sem_gr, sem1s, sem1r, sem2s, sem2r, sem3s, sem3r,
):
    me = lax.axis_index("member")
    cell = lax.axis_index("cell")
    core = lax.rem(cell, 2)
    grp = cell // 2
    G = CN // 2
    N, D = lat.shape
    H = w_in.shape[1]
    FD = w_out.shape[0]
    C = N // M
    PB = M // 2
    r = D // (M * CN)
    scale = 1.0 / (float(N * CN) ** 0.5) / M

    def block_of(i):
        return lax.rem(me // 2 + 1 + i, PB)

    def load(i):
        rows = pl.ds(pl.multiple_of(block_of(i) * (2 * C), 2 * C), 2 * C)
        return pltpu.make_async_copy(lat_hbm.at[rows, :], lat.at[rows, :], sem_in.at[i])

    load_w = pltpu.make_async_copy(w_in_hbm, w_in, sem_in.at[PB])
    load_w.start()
    for i in range(PB):
        load(i).start()

    barrier = pltpu.get_barrier_semaphore()
    for d in range(1, M):
        pl.semaphore_signal(barrier, inc=1, device_id=(lax.rem(me + d, M), cell), device_id_type=MESH)
    pl.semaphore_signal(barrier, inc=1, device_id=(me, grp * 2 + 1 - core), device_id_type=MESH)
    for d in range(1, G):
        pl.semaphore_signal(
            barrier, inc=1, device_id=(me, lax.rem(grp + d, G) * 2 + core), device_id_type=MESH
        )

    for b in range(N // 128):
        cols = slice(128 * b, 128 * b + 128)
        tgt_t[cols, :] = target[:, cols].astype(F32).T
        w = mask[cols].astype(F32) * scale
        wgt_t[cols, :] = jnp.broadcast_to(w[None, :], (8, 128)).T

    pl.semaphore_wait(barrier, M - 1 + 1 + G - 1)

    def peer(d):
        return lax.rem(me + d, M)

    def f_copy(d):
        return pltpu.make_async_remote_copy(
            fsend.at[peer(d)], frecv.at[d - 1], sem_fs.at[d - 1], sem_fr.at[d - 1],
            device_id=(peer(d), cell), device_id_type=MESH,
        )

    def g_copy(d):
        return pltpu.make_async_remote_copy(
            gsend.at[d - 1], gf.at[me], sem_gs.at[d - 1], sem_gr.at[d - 1],
            device_id=(lax.rem(me - d + M, M), cell), device_id_type=MESH,
        )

    def c1(i):
        return pltpu.make_async_remote_copy(
            acc_b.at[i, 1 - core], r1.at[i], sem1s.at[i], sem1r.at[i],
            device_id=(me, grp * 2 + 1 - core), device_id_type=MESH,
        )

    def c2(i, d):
        g = lax.rem(grp + d, G)
        return pltpu.make_async_remote_copy(
            s2.at[i, g], r2.at[i, d - 1], sem2s.at[i, d - 1], sem2r.at[i, d - 1],
            device_id=(me, g * 2 + core), device_id_type=MESH,
        )

    def c3(t):
        d = lax.rem(t - me + M, M)
        return pltpu.make_async_remote_copy(
            s3.at[t], r3.at[d - 1], sem3s.at[d - 1], sem3r.at[d - 1],
            device_id=(t, cell), device_id_type=MESH,
        )

    def forward(i, carry):
        p = block_of(i)
        rows = pl.ds(pl.multiple_of(p * (2 * C), 2 * C), 2 * C)
        load(i).wait()
        v = mm(lat[rows, :], w_in[...])
        s = sigmoid(v)
        slope[rows, :] = s * (1.0 + v * (1.0 - s))
        h = (v * s).astype(BF)
        hid[rows, :] = h
        f = lax.dot_general(
            h, w_out[...], (((1,), (1,)), ((), ())), preferred_element_type=F32
        ).astype(BF)
        fsend[2 * p] = f[:C]
        fsend[2 * p + 1] = f[C:]
        for s in range(2):
            t = 2 * p + s

            @pl.when(t != me)
            def _():
                f_copy(lax.rem(t - me + M, M)).start()

        return carry

    load_w.wait()
    lax.fori_loop(0, PB, forward, 0)

    for b in range(N // 128):
        cols = slice(128 * b, 128 * b + 128)
        lat_t[:, cols] = lat[cols, :].T

    for d in range(1, M):
        f_copy(d).wait_recv()

    RB = 16

    def pairs(b, carry):
        rows = pl.ds(pl.multiple_of(b * RB, RB), RB)
        own = pl.ds(pl.multiple_of(me * C + b * RB, RB), RB)
        vals = [frecv[j, rows, :].astype(F32) for j in range(M - 1)]
        vals.append(fsend[me, rows, :].astype(F32))
        t = tgt_t[own, :]
        w = wgt_t[own, 0:1]
        total = [None] * M
        for a in range(M):
            for c in range(a + 1, M):
                k = smooth(vals[a] - vals[c])
                total[a] = k if total[a] is None else total[a] + k
                total[c] = -k if total[c] is None else total[c] - k
        for a in range(M):
            g = (w * (smooth(vals[a] - t) - total[a] * (1.0 / M))).astype(BF)
            if a < M - 1:
                gsend[a, rows, :] = g
            else:
                gf[me, rows, :] = g
        return carry

    lax.fori_loop(0, C // RB, pairs, 0)

    for d in range(1, M):
        g_copy(d).start()

    for b in range(N // 128):
        cols = slice(128 * b, 128 * b + 128)
        hid_t[:, cols] = hid[cols, :].T

    def back(j):
        rows = pl.ds(pl.multiple_of(j * C, C), C)
        gp[rows, :] = (mm(gf[j], w_out[...]) * slope[rows, :]).astype(BF)

    back(me)

    def backs(d, carry):
        pltpu.make_async_remote_copy(
            gsend.at[d - 1], gf.at[lax.rem(me + d, M)], sem_gs.at[d - 1], sem_gr.at[d - 1],
            device_id=(peer(d), cell), device_id_type=MESH,
        ).wait_recv()
        back(lax.rem(me + d, M))
        return carry

    lax.fori_loop(1, M, backs, 0)

    def step(i, carry):
        @pl.when(i < PB)
        def _():
            p = block_of(i)
            rows = pl.ds(pl.multiple_of(p * (2 * r * CN), 2 * r * CN), 2 * r * CN)
            a = mm(lat_t[rows, :], gp[...])
            b = mm(hid_t[rows, :], gf[...].reshape(N, FD))
            for s in range(2):
                for c in range(CN):
                    at = (s * CN + c) * r
                    x, y = a[at : at + r], b[at : at + r]
                    acc_f[i, c % 2, s, c // 2, :, :H] = x
                    acc_f[i, c % 2, s, c // 2, :, H : H + FD] = y
                    acc_b[i, c % 2, s, c // 2, :, :H] = x.astype(BF)
                    acc_b[i, c % 2, s, c // 2, :, H : H + FD] = y.astype(BF)
            c1(i).start()

        @pl.when((i >= 1) & (i <= PB))
        def _():
            j = i - 1
            c1(j).wait_recv()
            for g in range(G):
                for s in range(2):
                    v = acc_f[j, core, s, g] + r1[j, s, g].astype(F32)
                    k2[j, g, s] = v
                    s2[j, g, s] = v.astype(BF)
            for d in range(1, G):
                c2(j, d).start()

        @pl.when(i >= 2)
        def _():
            j = i - 2
            p = block_of(j)
            for d in range(1, G):
                c2(j, d).wait_recv()
            for s in range(2):
                v = k2[j, grp, s]
                for d in range(1, G):
                    v = v + r2[j, d - 1, s].astype(F32)
                t = 2 * p + s
                s3[t] = v.astype(BF)

                @pl.when(t == me)
                def _():
                    k3[...] = v

                @pl.when(t != me)
                def _():
                    c3(t).start()

        return carry

    lax.fori_loop(0, PB + 2, step, 0)

    total = k3[...]
    for d in range(1, M):
        pltpu.make_async_remote_copy(
            s3.at[0], r3.at[d - 1], sem3s.at[d - 1], sem3r.at[d - 1],
            device_id=(peer(d), cell), device_id_type=MESH,
        ).wait_recv()
        total = total + r3[d - 1].astype(F32)
    out_in[...] = total[:, :H]
    out_out[...] = total[:, H : H + FD]

    for d in range(1, M):
        f_copy(d).wait_send()
        g_copy(d).wait_send()
        c3(peer(d)).wait_send()
    for i in range(PB):
        c1(i).wait_send()
        for d in range(1, G):
            c2(i, d).wait_send()


def per_device(latent, w_in, w_out, target, cell_mask):
    M = lax.axis_size("member")
    CN = lax.axis_size("cell")
    N, D = latent.shape[1:]
    H = w_in.shape[1]
    FD = w_out.shape[1]
    C, PB, G = N // M, M // 2, CN // 2
    r = D // (M * CN)
    W = H + (FD + 127) // 128 * 128
    V = pltpu.VMEM
    DMA = pltpu.SemaphoreType.DMA
    GS = max(G - 1, 1)
    vm = pl.BlockSpec(memory_space=pltpu.VMEM)
    return pl.pallas_call(
        functools.partial(body, M, CN),
        out_shape=(
            jax.ShapeDtypeStruct((r, H), F32),
            jax.ShapeDtypeStruct((r, FD), F32),
        ),
        in_specs=[pl.BlockSpec(memory_space=pl.ANY)] * 2 + [vm] * 3,
        out_specs=(vm, vm),
        scratch_shapes=[
            V((N, D), BF), V((D, H), BF), V((N, H), F32), V((N, H), BF), V((N, H), BF), V((D, N), BF), V((H, N), BF),
            V((N, FD), F32), V((N, 8), F32),
            V((M, C, FD), BF), V((M - 1, C, FD), BF), V((M - 1, C, FD), BF), V((M, C, FD), BF),
            V((PB, 2, 2, G, r, W), F32), V((PB, 2, 2, G, r, W), BF), V((PB, 2, G, r, W), BF),
            V((PB, G, 2, r, W), F32), V((PB, G, 2, r, W), BF), V((PB, GS, 2, r, W), BF),
            V((M, r, W), BF), V((M - 1, r, W), BF), V((r, W), F32),
            DMA((PB + 1,)), DMA((M - 1,)), DMA((M - 1,)), DMA((M - 1,)), DMA((M - 1,)),
            DMA((PB,)), DMA((PB,)), DMA((PB, GS)), DMA((PB, GS)),
            DMA((M - 1,)), DMA((M - 1,)),
        ],
        compiler_params=pltpu.CompilerParams(
            collective_id=0, has_side_effects=True, vmem_limit_bytes=60 * 1024 * 1024
        ),
    )(latent[0], w_in, w_out.T, target, cell_mask)


def solution(mesh):
    in_specs = (P("member", "cell", None), P(), P(), P(None, "cell"), P("cell"))
    out_specs = (P(("member", "cell"), None), P(("member", "cell"), None))
    return jax.shard_map(
        per_device, mesh=mesh, in_specs=in_specs, out_specs=out_specs, check_vma=False
    )
```

profile of v0, /device:TPU:0, one launch (start us, length us, event | category | flops | bytes accessed | tf_op | source)
XLA Modules:
  0.0 55.2 jit_solution(1186528827216810116)
XLA Ops:
  0.6 51.7 %shard_map.68 = (f32[32,1024]{1,0:T(8,128)}, f32[32,96]{1,0:T(8,128)}) custom-call(bf16[1536,1024]{1,0:T(8,128)(2,1)} %bitcast.2, bf16[1024,1024]{1,0:T(8,128)(2,1)} %w_in_hbm.1, bf16[96,1024]{1,0:T(8,128)(2,1)} %bitcast.3, bf16[96,1536]{1,0:T(8,128)(2,1)} %target.1, s32[1536]{0:T(1024)} %mask.1), custom_call_target="tpu_custom_call" | custom-call | tf_op jit(solution)/shard_map/pallas_call | solution.py:280
  52.3 1.6 %copy.9 = f32[32,1024]{1,0:T(8,128)} copy(f32[32,1024]{1,0:T(8,128)} %get-tuple-element.4) | data formatting | bytes 262144
  53.9 1.3 %copy.10 = f32[32,96]{1,0:T(8,128)} copy(f32[32,96]{1,0:T(8,128)} %get-tuple-element.5) | data formatting | bytes 24576
where the time goes:
time: 55.5 us; the launch traced here: 55.2 us
  Pallas kernels  51.7 us (93%)
  local copies, waits for them, and re-layouts  2.89 us (5%)
  between operations  0.64 us (1%)
    pallas_call x1, Pallas kernels, per_device(): pl.pallas_call(functools.partial(body, M, CN), out_shape=(jax.ShapeDtypeS...  51.7 us
    unnamed x2, local copies, waits for them, and re-layouts  2.89 us

commit v1 on v0

v1 whole, which is shorter than its diff:
```python
import functools
import math

import jax
import jax.numpy as jnp
from jax import lax
from jax.experimental import pallas as pl
from jax.experimental.pallas import tpu as pltpu
from jax.sharding import PartitionSpec as P

MESH = pl.DeviceIdType.MESH
BF = jnp.bfloat16
F32 = jnp.float32
LANES = 128
PHASES = 3


def sigmoid(v):
    return 0.5 * jnp.tanh(0.5 * v) + 0.5


def smooth(d):
    return d * lax.rsqrt(1.0 + d * d)


def mm(a, b):
    return jnp.dot(a, b, preferred_element_type=F32)


def pack(f, width):
    spare = LANES - width
    n = width // spare
    q = f.shape[0] // (n + 1)
    lane = lax.broadcasted_iota(jnp.int32, (q, LANES), 1)
    last = f[n * q :]
    parts = []
    for k in range(n):
        parts.append(jnp.where(lane < width, f[k * q : (k + 1) * q], pltpu.roll(last, width - spare * k, 1)))
    return jnp.concatenate(parts, axis=0)


def unpack_last(p, width):
    spare = LANES - width
    n = width // spare
    q = p.shape[0] // n
    lane = lax.broadcasted_iota(jnp.int32, (q, LANES), 1)
    out = pltpu.roll(p[:q], spare, 1)
    for k in range(1, n):
        out = jnp.where(lane < spare * k, out, pltpu.roll(p[k * q : (k + 1) * q], spare * (k + 1), 1))
    return out


def body(
    M, CN, WA,
    lat_hbm, w_in_hbm, w_out_hbm, target_hbm, mask_hbm, out,
    lat, w_in, wo, target, mask, slope, hid, gp, gfu, lat_t, hid_t, tgt_t, wgt_t,
    fsend, frecv, gsend, gf,
    acc, acc_f, acc_b, r1, k2, a2, b2, ra, rb, k3, a3, b3, r3a, r3b, sz, rz,
    sem_in, sem_fs, sem_fr, sem_gs, sem_gr,
    sem1s, sem1r, sem2as, sem2ar, sem2bs, sem2br, sem3as, sem3ar, sem3bs, sem3br, sem4s, sem4r,
):
    me = lax.axis_index("member")
    cell = lax.axis_index("cell")
    core = lax.rem(cell, 2)
    grp = cell // 2
    G = CN // 2
    HM = M // 2
    PB = M // 2
    z = me // 2
    x = lax.rem(me, 2)
    half = me // HM
    PH = fsend.shape[0]
    CH, D = lat.shape[2:]
    H = w_in.shape[1]
    FD = w_out_hbm.shape[0]
    B = HM * CH
    K = M * CH
    C = PH * CH
    N = PH * K
    PR = fsend.shape[2]
    W = acc.shape[2]
    r = D // (M * CN)
    scale = 1.0 / (float(N * CN) ** 0.5) / M
    pair_core = (me, grp * 2 + 1 - core)
    pair_x = (me + 1 - 2 * x, cell)

    barrier = pltpu.get_barrier_semaphore()
    for d in range(1, M):
        pl.semaphore_signal(barrier, inc=1, device_id=(lax.rem(me + d, M), cell), device_id_type=MESH)
    pl.semaphore_signal(barrier, inc=1, device_id=pair_core, device_id_type=MESH)
    for d in range(1, G):
        pl.semaphore_signal(
            barrier, inc=1, device_id=(me, lax.rem(grp + d, G) * 2 + core), device_id_type=MESH
        )

    def which_half(i):
        return (1 - half) * (1 - lax.rem(i, 2)) + half * lax.rem(i, 2)

    def load(i):
        h = i // 2
        hf = which_half(i)
        return pltpu.make_async_copy(
            lat_hbm.at[pl.ds(hf * HM, HM), pl.ds(pl.multiple_of(h * CH, CH), CH), :],
            lat.at[2 * h + hf],
            sem_in.at[i],
        )

    load_w = pltpu.make_async_copy(w_in_hbm, w_in, sem_in.at[2 * PH])
    load_o = pltpu.make_async_copy(w_out_hbm, wo.at[pl.ds(0, FD), :], sem_in.at[2 * PH + 1])
    load_t = pltpu.make_async_copy(target_hbm, target, sem_in.at[2 * PH + 2])
    load_m = pltpu.make_async_copy(mask_hbm, mask, sem_in.at[2 * PH + 3])
    load_w.start()
    load(0).start()
    load_o.start()
    for i in range(1, 2 * PH):
        load(i).start()
    load_t.start()
    load_m.start()
    wo[FD:, :] = jnp.zeros((LANES - FD, H), BF)

    def f_copy(h, t):
        return pltpu.make_async_remote_copy(
            fsend.at[h, t], frecv.at[h, me], sem_fs.at[h, t], sem_fr.at[h, me],
            device_id=(t, cell), device_id_type=MESH,
        )

    def f_wait(h, j):
        pltpu.make_async_remote_copy(
            fsend.at[h, j], frecv.at[h, j], sem_fs.at[h, j], sem_fr.at[h, j],
            device_id=(j, cell), device_id_type=MESH,
        ).wait_recv()

    def g_copy(h, t):
        return pltpu.make_async_remote_copy(
            gsend.at[h, t], gf.at[h, me], sem_gs.at[h, t], sem_gr.at[h, me],
            device_id=(t, cell), device_id_type=MESH,
        )

    def g_wait(h, j):
        pltpu.make_async_remote_copy(
            gsend.at[h, j], gf.at[h, j], sem_gs.at[h, j], sem_gr.at[h, j],
            device_id=(j, cell), device_id_type=MESH,
        ).wait_recv()

    def other_half(k):
        return (1 - half) * HM + lax.rem(me + k, HM)

    def same_half(k):
        return half * HM + lax.rem(me + k, HM)

    def c1(i):
        return pltpu.make_async_remote_copy(
            acc_b.at[i, 1 - core], r1.at[i], sem1s.at[i], sem1r.at[i],
            device_id=pair_core, device_id_type=MESH,
        )

    def c2a(i, d):
        g = lax.rem(grp + d, G)
        return pltpu.make_async_remote_copy(
            a2.at[i, g], ra.at[i, d - 1], sem2as.at[i, d - 1], sem2ar.at[i, d - 1],
            device_id=(me, g * 2 + core), device_id_type=MESH,
        )

    def c2b(i):
        return pltpu.make_async_remote_copy(
            b2.at[i, 1 - x], rb.at[i], sem2bs.at[i], sem2br.at[i],
            device_id=pair_x, device_id_type=MESH,
        )

    def c3a(i):
        return pltpu.make_async_remote_copy(
            a3.at[i], r3a.at[i], sem3as.at[i], sem3ar.at[i],
            device_id=pair_x, device_id_type=MESH,
        )

    def c3b(i, d):
        g = lax.rem(grp + d, G)
        return pltpu.make_async_remote_copy(
            b3.at[i, g], r3b.at[i, d - 1], sem3bs.at[i, d - 1], sem3br.at[i, d - 1],
            device_id=(me, g * 2 + core), device_id_type=MESH,
        )

    def block_of(i):
        return lax.rem(z + 1 + i, PB)

    def c4(i):
        return pltpu.make_async_remote_copy(
            sz.at[i], rz.at[i], sem4s.at[i], sem4r.at[i],
            device_id=(block_of(i) * 2 + x, cell), device_id_type=MESH,
        )

    def forward(i, carry):
        h = i // 2
        hf = which_half(i)
        blk = 2 * h + hf
        rows = pl.ds(pl.multiple_of(blk * B, B), B)
        load(i).wait()
        v = mm(lat[blk].reshape(B, D), w_in[...])
        s = sigmoid(v)
        slope[rows, :] = s * (1.0 + v * (1.0 - s))
        hb = (v * s).astype(BF)
        hid[rows, :] = hb
        f = lax.dot_general(hb, wo[...], (((1,), (1,)), ((), ())), preferred_element_type=F32)

        @pl.when(i == 0)
        def _():
            pl.semaphore_wait(barrier, M - 1 + 1 + G - 1)

        for k in range(HM):
            t = hf * HM + k
            p = pack(f[k * CH : (k + 1) * CH], FD).astype(BF)
            fsend[h, t] = p

            @pl.when(t == me)
            def _():
                frecv[h, me] = p

            @pl.when(t != me)
            def _():
                f_copy(h, t).start()

        return carry

    with jax.named_scope("loadw"):
        load_w.wait()
        load_o.wait()
    with jax.named_scope("forward"):
        lax.fori_loop(0, 2 * PH, forward, 0)

    with jax.named_scope("prep"):
        load_t.wait()
        load_m.wait()
        NB = tgt_t.shape[0] // LANES
        b0 = jnp.minimum(me * C // LANES, N // LANES - NB)
        for b in range(NB):
            cols = pl.ds(pl.multiple_of((b0 + b) * LANES, LANES), LANES)
            tgt_t[b * LANES : (b + 1) * LANES, :FD] = target[:, cols].astype(F32).T
        for b in range(N // LANES):
            cols = slice(LANES * b, LANES * b + LANES)
            w = mask[cols].astype(F32) * scale
            wgt_t[cols, :] = jnp.broadcast_to(w[None, :], (8, LANES)).T
        for h in range(PH):
            for b in range(K // LANES):
                lat_t[h, :, LANES * b : LANES * b + LANES] = (
                    lat[2 * h : 2 * h + 2].reshape(K, D)[LANES * b : LANES * b + LANES, :].T
                )

    RB = 16 if PR % 16 == 0 else PR

    def phase(h, carry):
        for k in range(1, HM):
            f_wait(h, same_half(k))
        for k in range(HM):
            f_wait(h, other_half(k))
        own = pl.multiple_of(me * C - b0 * LANES + h * CH, 8)
        tp = pack(tgt_t[pl.ds(own, CH), :], FD)
        wp = pack(
            jnp.broadcast_to(wgt_t[pl.ds(pl.multiple_of(me * C + h * CH, 8), CH), 0:1], (CH, LANES)), FD
        )
        for b in range(PR // RB):
            rows = slice(b * RB, (b + 1) * RB)
            vals = [frecv[h, j, rows, :].astype(F32) for j in range(M)]
            total = [None] * M
            for a in range(M):
                for c in range(a + 1, M):
                    k = smooth(vals[a] - vals[c])
                    total[a] = k if total[a] is None else total[a] + k
                    total[c] = -k if total[c] is None else total[c] - k
            for a in range(M):
                g = wp[rows] * (smooth(vals[a] - tp[rows]) - total[a] * (1.0 / M))
                gsend[h, a, rows, :] = g.astype(BF)
        for k in range(HM):
            g_copy(h, other_half(k)).start()
        for k in range(1, HM):
            g_copy(h, same_half(k)).start()
        gf[h, me] = gsend[h, me]
        return carry

    with jax.named_scope("pairs"):
        lax.fori_loop(0, PH, phase, 0)

    with jax.named_scope("hidt"):
        for h in range(PH):
            for b in range(K // LANES):
                at = h * K + LANES * b
                hid_t[h, :, LANES * b : LANES * b + LANES] = hid[at : at + LANES, :].T

    def back(h, hf):
        blk = 2 * h + hf
        for k in range(HM):
            p = gf[h, hf * HM + k]
            at = pl.multiple_of(blk * B + k * CH, CH)
            gfu[pl.ds(at, PR), :] = p
            gfu[pl.ds(pl.multiple_of(at + PR, CH - PR), CH - PR), :] = unpack_last(p.astype(F32), FD).astype(BF)
        rows = pl.ds(pl.multiple_of(blk * B, B), B)
        gp[rows, :] = (mm(gfu[rows, :], wo[...]) * slope[rows, :]).astype(BF)

    def gather(h):
        for k in range(1, HM):
            g_wait(h, same_half(k))
        back(h, half)
        for k in range(HM):
            g_wait(h, other_half(k))
        back(h, 1 - half)

    def terms(h, p):
        rows = pl.ds(pl.multiple_of(p * (2 * r * CN), 2 * r * CN), 2 * r * CN)
        at = pl.ds(pl.multiple_of(h * K, K), K)
        return mm(lat_t[h, rows, :], gp[at, :]), mm(hid_t[h, rows, :], gfu[at, :])

    def early(h, carry):
        gather(h)

        def add(p, c):
            a, b = terms(h, p)

            @pl.when(h == 0)
            def _():
                acc[p, :, :H] = a
                acc[p, :, H:] = b

            @pl.when(h > 0)
            def _():
                acc[p, :, :H] += a
                acc[p, :, H:] += b

            return c

        return lax.fori_loop(0, PB, add, carry)

    with jax.named_scope("early"):
        lax.fori_loop(0, PH - 1, early, 0)

    with jax.named_scope("gather"):
        gather(PH - 1)

    def first(i, carry):
        p = block_of(i)
        a, b = terms(PH - 1, p)
        a = a + acc[p, :, :H]
        b = b + acc[p, :, H:]
        for s in range(2):
            for c in range(CN):
                at = (s * CN + c) * r
                u, v = a[at : at + r], b[at : at + r]
                acc_f[i, c % 2, s, c // 2, :, :H] = u
                acc_f[i, c % 2, s, c // 2, :, H:] = v
                acc_b[i, c % 2, s, c // 2, :, :H] = u.astype(BF)
                acc_b[i, c % 2, s, c // 2, :, H:] = v.astype(BF)
        c1(i).start()
        return carry

    with jax.named_scope("first"):
        lax.fori_loop(0, PB, first, 0)

    def second(i, carry):
        c1(i).wait_recv()
        for s in range(2):
            for g in range(G):
                v = acc_f[i, core, s, g] + r1[i, s, g].astype(F32)
                k2[i, s, g] = v
                a2[i, g, s] = v[:, :WA].astype(BF)
                b2[i, s, g] = v[:, WA:].astype(BF)
        for d in range(1, G):
            c2a(i, d).start()
        c2b(i).start()
        return carry

    with jax.named_scope("second"):
        lax.fori_loop(0, PB, second, 0)

    def third(i, carry):
        for d in range(1, G):
            c2a(i, d).wait_recv()
        away = k2[i, 1 - x, grp, :, :WA]
        keep = k2[i, x, grp, :, :WA]
        for d in range(1, G):
            away = away + ra[i, d - 1, 1 - x].astype(F32)
            keep = keep + ra[i, d - 1, x].astype(F32)
        a3[i] = away.astype(BF)
        c3a(i).start()
        k3[i, :, :WA] = keep
        c2b(i).wait_recv()
        for g in range(G):
            b3[i, g] = (k2[i, x, g, :, WA:] + rb[i, g].astype(F32)).astype(BF)
        for d in range(1, G):
            c3b(i, d).start()
        k3[i, :, WA:] = k2[i, x, grp, :, WA:] + rb[i, grp].astype(F32)
        return carry

    with jax.named_scope("third"):
        lax.fori_loop(0, PB, third, 0)

    def fourth(i, carry):
        c3a(i).wait_recv()
        u = k3[i, :, :WA] + r3a[i].astype(F32)
        v = k3[i, :, WA:]
        for d in range(1, G):
            c3b(i, d).wait_recv()
            v = v + r3b[i, d - 1].astype(F32)

        @pl.when(i < PB - 1)
        def _():
            sz[i, :, :WA] = u.astype(BF)
            sz[i, :, WA:] = v.astype(BF)
            c4(i).start()

        @pl.when(i == PB - 1)
        def _():
            out[:, :WA] = u
            out[:, WA:] = v

        return carry

    with jax.named_scope("fourth"):
        lax.fori_loop(0, PB, fourth, 0)

    with jax.named_scope("last"):
        total = out[...]
        for i in range(PB - 1):
            c4(i).wait_recv()
            total = total + rz[i].astype(F32)
        out[...] = total

    for h in range(PH):
        for k in range(HM):
            f_copy(h, other_half(k)).wait_send()
            g_copy(h, other_half(k)).wait_send()
        for k in range(1, HM):
            f_copy(h, same_half(k)).wait_send()
            g_copy(h, same_half(k)).wait_send()
    for i in range(PB):
        c1(i).wait_send()
        for d in range(1, G):
            c2a(i, d).wait_send()
            c3b(i, d).wait_send()
        c2b(i).wait_send()
        c3a(i).wait_send()
        if i < PB - 1:
            c4(i).wait_send()


def split(res, out_in, out_out):
    H = out_in.shape[1]
    out_in[...] = res[:, :H]
    out_out[...] = res[:, H : H + out_out.shape[1]]


def per_device(latent, w_in, w_out, target, cell_mask):
    M = lax.axis_size("member")
    CN = lax.axis_size("cell")
    N, D = latent.shape[1:]
    H = w_in.shape[1]
    FD = w_out.shape[1]
    PH = PHASES
    C = N // M
    CH = C // PH
    K = M * CH
    PB, G = M // 2, CN // 2
    n = FD // (LANES - FD)
    PR = CH // (n + 1) * n
    r = D // (M * CN)
    W = H + LANES
    WA = (W // LANES + 1) // 2 * LANES
    WB = W - WA
    NB = -(-(LANES - math.gcd(C, LANES) + C) // LANES)
    GS = max(G - 1, 1)
    V = pltpu.VMEM
    DMA = pltpu.SemaphoreType.DMA
    vm = pl.BlockSpec(memory_space=pltpu.VMEM)
    res = pl.pallas_call(
        functools.partial(body, M, CN, WA),
        out_shape=jax.ShapeDtypeStruct((r, W), F32),
        in_specs=[pl.BlockSpec(memory_space=pl.ANY)] * 5,
        out_specs=vm,
        scratch_shapes=[
            V((2 * PH, M // 2, CH, D), BF), V((D, H), BF), V((LANES, H), BF), V((FD, N), BF), V((N,), jnp.int32),
            V((N, H), F32), V((N, H), BF), V((N, H), BF), V((N, LANES), BF), V((PH, D, K), BF), V((PH, H, K), BF),
            V((NB * LANES, LANES), F32), V((N, 8), F32),
            V((PH, M, PR, LANES), BF), V((PH, M, PR, LANES), BF), V((PH, M, PR, LANES), BF), V((PH, M, PR, LANES), BF),
            V((PB, 2 * CN * r, W), F32), V((PB, 2, 2, G, r, W), F32), V((PB, 2, 2, G, r, W), BF), V((PB, 2, G, r, W), BF),
            V((PB, 2, G, r, W), F32), V((PB, G, 2, r, WA), BF), V((PB, 2, G, r, WB), BF),
            V((PB, GS, 2, r, WA), BF), V((PB, G, r, WB), BF),
            V((PB, r, W), F32), V((PB, r, WA), BF), V((PB, G, r, WB), BF), V((PB, r, WA), BF), V((PB, GS, r, WB), BF),
            V((PB, r, W), BF), V((PB, r, W), BF),
            DMA((2 * PH + 4,)), DMA((PH, M)), DMA((PH, M)), DMA((PH, M)), DMA((PH, M)),
            DMA((PB,)), DMA((PB,)), DMA((PB, GS)), DMA((PB, GS)), DMA((PB,)), DMA((PB,)),
            DMA((PB,)), DMA((PB,)), DMA((PB, GS)), DMA((PB, GS)), DMA((PB,)), DMA((PB,)),
        ],
        compiler_params=pltpu.CompilerParams(
            collective_id=0, has_side_effects=True, vmem_limit_bytes=60 * 1024 * 1024
        ),
    )(latent.reshape(M, C, D), w_in, w_out.T, target, cell_mask)
    return pl.pallas_call(
        split,
        out_shape=(jax.ShapeDtypeStruct((r, H), F32), jax.ShapeDtypeStruct((r, FD), F32)),
        in_specs=[vm],
        out_specs=(vm, vm),
    )(res)


def solution(mesh):
    in_specs = (P("member", "cell", None), P(), P(), P(None, "cell"), P("cell"))
    out_specs = (P(("member", "cell"), None), P(("member", "cell"), None))
    return jax.shard_map(
        per_device, mesh=mesh, in_specs=in_specs, out_specs=out_specs, check_vma=False
    )
```

time: 55.5 us -> 51.6 us (0.930)
  local copies, waits for them, and re-layouts: 2.89 us -> 0 us
  Pallas kernels: 51.7 us -> 50.8 us
    unnamed x2 -> x0, local copies, waits for them, and re-layouts: 2.89 us -> none
    pallas_call x1 -> x2, Pallas kernels: 51.7 us -> 50.8 us  [the longest x1 49.3 us: per_device(): pl.pallas_call(functools.partial(body, M, CN, WA), out_shape=jax.ShapeDty...]
where the time goes in v1:
time: 51.6 us; the launch traced here: 51.5 us
  Pallas kernels  50.8 us (98%)
  between operations  0.64 us (1%)
    pallas_call x1, Pallas kernels, per_device(): pl.pallas_call(functools.partial(body, M, CN, WA), out_shape=jax.ShapeDty...  49.3 us
    pallas_call x1, Pallas kernels, per_device(): pl.pallas_call(split, out_shape=(jax.ShapeDtypeStruct((r, H), F32), jax.S...  1.58 us

profile of v1, /device:TPU:0, one launch (start us, length us, event | category | flops | bytes accessed | tf_op | source)
XLA Modules:
  0.0 51.5 jit_solution(12209235708706311337)
XLA Ops:
  0.6 49.3 %shard_map.68.res = f32[32,1152]{1,0:T(8,128)} custom-call(bf16[8,192,1024]{2,1,0:T(8,128)(2,1)} %bitcast.2, bf16[1024,1024]{1,0:T(8,128)(2,1)} %w_in_hbm.1, bf16[96,1024]{1,0:T(8,128)(2,1)} %bitcast.3, bf16[96,1536]{1,0:T(8,128)(2,1)} %target_hbm.1, s32[1536]{0:T(1024)} %mask_hbm.1), custom_call_target="tpu_custom_call" | custom-call | tf_op jit(solution)/shard_map/pallas_call | solution.py:471
  49.9 1.6 %shard_map.69 = (f32[32,1024]{1,0:T(8,128)}, f32[32,96]{1,0:T(8,128)}) custom-call(f32[32,1152]{1,0:T(8,128)} %shard_map.68.res), custom_call_target="tpu_custom_call" | custom-call | tf_op jit(solution)/shard_map/pallas_call | solution.py:494

commit v2 on v1

v2 whole, which is shorter than its diff:
```python
import functools
import math

import jax
import jax.numpy as jnp
from jax import lax
from jax.experimental import pallas as pl
from jax.experimental.pallas import tpu as pltpu
from jax.sharding import PartitionSpec as P

MESH = pl.DeviceIdType.MESH
BF = jnp.bfloat16
F32 = jnp.float32
LANES = 128
PHASES = 3


def smooth(d):
    return d * lax.rsqrt(1.0 + d * d)


def mm(a, b):
    return jnp.dot(a, b, preferred_element_type=F32)


def pack(f, width):
    spare = LANES - width
    n = width // spare
    q = f.shape[0] // (n + 1)
    lane = lax.broadcasted_iota(jnp.int32, (q, LANES), 1)
    last = f[n * q :]
    parts = []
    for k in range(n):
        parts.append(jnp.where(lane < width, f[k * q : (k + 1) * q], pltpu.roll(last, width - spare * k, 1)))
    return jnp.concatenate(parts, axis=0)


def unpack_last(p, width):
    spare = LANES - width
    n = width // spare
    q = p.shape[0] // n
    lane = lax.broadcasted_iota(jnp.int32, (q, LANES), 1)
    out = pltpu.roll(p[:q], spare, 1)
    for k in range(1, n):
        out = jnp.where(lane < spare * k, out, pltpu.roll(p[k * q : (k + 1) * q], spare * (k + 1), 1))
    return out


def body(
    M, CN, chunks,
    lat_hbm, w_in_hbm, w_out_hbm, target_hbm, mask_hbm, out_in, out_out,
    lat, w_in, wo, wh, target, mask, slope, hid, gp, gfu, lat_t, hid_t, tgt_t, wgt_t,
    fsend, frecv, gsend, gf,
    acc, kf, sb, r1, s2, r2a, r2b, k3, s3a, r3a, s3b, r3b, sz, rz,
    sem_in, sem_fs, sem_fr, sem_gs, sem_gr,
    sem1s, sem1r, sem2as, sem2ar, sem2bs, sem2br, sem3as, sem3ar, sem3bs, sem3br, sem4s, sem4r,
):
    me = lax.axis_index("member")
    cell = lax.axis_index("cell")
    core = lax.rem(cell, 2)
    grp = cell // 2
    G = CN // 2
    HM = M // 2
    PB = M // 2
    z = me // 2
    x = lax.rem(me, 2)
    half = me // HM
    near, far = half * HM, (1 - half) * HM
    PH = fsend.shape[0]
    CH, D = lat.shape[2:]
    H = w_in.shape[1]
    FD = w_out_hbm.shape[0]
    B = HM * CH
    K = M * CH
    C = PH * CH
    N = PH * K
    PR = fsend.shape[2]
    W = acc.shape[2]
    r = D // (M * CN)
    scale = 1.0 / (float(N * CN) ** 0.5) / M
    pair_core = (me, grp * 2 + 1 - core)
    pair_x = (me + 1 - 2 * x, cell)

    barrier = pltpu.get_barrier_semaphore()
    for d in range(1, M):
        pl.semaphore_signal(barrier, inc=1, device_id=(lax.rem(me + d, M), cell), device_id_type=MESH)
    pl.semaphore_signal(barrier, inc=1, device_id=pair_core, device_id_type=MESH)
    for d in range(1, G):
        pl.semaphore_signal(
            barrier, inc=1, device_id=(me, lax.rem(grp + d, G) * 2 + core), device_id_type=MESH
        )

    def load(rel, h):
        return pltpu.make_async_copy(
            lat_hbm.at[pl.ds(near if rel else far, HM), pl.ds(h * CH, CH), :],
            lat.at[rel * PH + h],
            sem_in.at[rel * PH + h],
        )

    load_w = pltpu.make_async_copy(w_in_hbm, w_in, sem_in.at[2 * PH])
    load_o = pltpu.make_async_copy(w_out_hbm, wo.at[pl.ds(0, FD), :], sem_in.at[2 * PH + 1])
    load_t = pltpu.make_async_copy(target_hbm, target, sem_in.at[2 * PH + 2])
    load_m = pltpu.make_async_copy(mask_hbm, mask, sem_in.at[2 * PH + 3])
    load_w.start()
    load(0, 0).start()
    load_o.start()
    for i in range(1, 2 * PH):
        load(i // PH, i % PH).start()
    load_t.start()
    load_m.start()
    wo[FD:, :] = jnp.zeros((LANES - FD, H), BF)

    def f_copy(h, t):
        return pltpu.make_async_remote_copy(
            fsend.at[h, t], frecv.at[h, me], sem_fs.at[0], sem_fr.at[h],
            device_id=(t, cell), device_id_type=MESH,
        )

    def g_copy(h, t, rel):
        return pltpu.make_async_remote_copy(
            gsend.at[h, t], gf.at[h, me], sem_gs.at[0], sem_gr.at[rel, h],
            device_id=(t, cell), device_id_type=MESH,
        )

    def arrived(ref, sem):
        pltpu.make_async_copy(ref, ref, sem).wait()

    def same_half(k):
        return near + lax.rem(me + k, HM)

    def c1(i):
        return pltpu.make_async_remote_copy(
            sb.at[i], r1.at[i], sem1s.at[0], sem1r.at[i], device_id=pair_core, device_id_type=MESH
        )

    def c2a(i, q, d):
        cols = pl.ds(chunks[q][0], chunks[q][1] - chunks[q][0])
        g = lax.rem(grp + d, G)
        return pltpu.make_async_remote_copy(
            s2.at[i, :, g, :, cols], r2a.at[i, d - 1, :, :, cols], sem2as.at[0], sem2ar.at[q, i, d - 1],
            device_id=(me, g * 2 + core), device_id_type=MESH,
        )

    def c2b(i, q):
        cols = pl.ds(chunks[q][1], chunks[q][2] - chunks[q][1])
        return pltpu.make_async_remote_copy(
            s2.at[i, 1 - x, :, :, cols], r2b.at[i, :, :, cols], sem2bs.at[0], sem2br.at[q, i],
            device_id=pair_x, device_id_type=MESH,
        )

    def c3a(i, q):
        cols = pl.ds(chunks[q][0], chunks[q][1] - chunks[q][0])
        return pltpu.make_async_remote_copy(
            s3a.at[i, :, cols], r3a.at[i, :, cols], sem3as.at[0], sem3ar.at[q, i],
            device_id=pair_x, device_id_type=MESH,
        )

    def c3b(i, q, d):
        cols = pl.ds(chunks[q][1], chunks[q][2] - chunks[q][1])
        g = lax.rem(grp + d, G)
        return pltpu.make_async_remote_copy(
            s3b.at[i, g, :, cols], r3b.at[i, d - 1, :, cols], sem3bs.at[0], sem3br.at[q, i, d - 1],
            device_id=(me, g * 2 + core), device_id_type=MESH,
        )

    HP = PB // 2
    zh = z // HP

    def block_of(i):
        far = (1 - zh) * HP + lax.rem(z + i + 1, HP)
        near = zh * HP + lax.rem(z + i + 1, HP)
        return jnp.where(i < HP, far, near)

    def c4(i, q):
        cols = pl.ds(chunks[q][0], chunks[q][2] - chunks[q][0])
        return pltpu.make_async_remote_copy(
            sz.at[i, :, cols], rz.at[i, :, cols], sem4s.at[0], sem4r.at[0],
            device_id=(block_of(i) * 2 + x, cell), device_id_type=MESH,
        )

    def decode(rel, h0, blocks):
        at = rel * PH + h0
        rows = slice(at * B, (at + blocks) * B)
        for h in range(h0, h0 + blocks):
            load(rel, h).wait()
        v = mm(lat[at : at + blocks].reshape(blocks * B, D), w_in[...])
        u = 0.5 * v
        t = jnp.tanh(u)
        ut = u * t
        hb = (u + ut).astype(BF)
        slope[rows, :] = (1.0 + t) + (u - ut * t)
        hid[rows, :] = hb
        return lax.dot_general(hb, wo[...], (((1,), (1,)), ((), ())), preferred_element_type=F32)

    def send_fields(rel, h0, blocks, f):
        for h in range(h0, h0 + blocks):
            for k in range(HM):
                at = ((h - h0) * HM + k) * CH
                t = (near if rel else far) + k
                fsend[h, t] = pack(f[at : at + CH], FD).astype(BF)
                if not rel:
                    f_copy(h, t).start()
            if rel:
                frecv[h, me] = fsend[h, me]
                for k in range(1, HM):
                    f_copy(h, same_half(k)).start()

    with jax.named_scope("forward"):
        load_w.wait()
        load_o.wait()
        f = decode(0, 0, 1)
        pl.semaphore_wait(barrier, M - 1 + 1 + G - 1)
        send_fields(0, 0, 1, f)
        send_fields(0, 1, PH - 1, decode(0, 1, PH - 1))
        send_fields(1, 0, 1, decode(1, 0, 1))
        send_fields(1, 1, PH - 1, decode(1, 1, PH - 1))

    with jax.named_scope("prep"):
        load_t.wait()
        load_m.wait()
        wh[...] = (0.5 * wo[...].astype(F32)).astype(BF)
        NB = tgt_t.shape[0] // LANES
        b0 = jnp.minimum(me * C // LANES, N // LANES - NB)
        for b in range(NB):
            cols = pl.ds(pl.multiple_of((b0 + b) * LANES, LANES), LANES)
            tgt_t[b * LANES : (b + 1) * LANES, :FD] = target[:, cols].astype(F32).T
        for b in range(N // LANES):
            cols = slice(LANES * b, LANES * b + LANES)
            w = mask[cols].astype(F32) * scale
            wgt_t[cols, :] = jnp.broadcast_to(w[None, :], (8, LANES)).T

    RB = 16 if PR % 16 == 0 else PR

    def phase(h, carry):
        arrived(frecv.at[h, pl.ds(0, M - 1)], sem_fr.at[h])
        own = pl.multiple_of(me * C - b0 * LANES + h * CH, 8)
        tp = pack(tgt_t[pl.ds(own, CH), :], FD)
        wp = pack(
            jnp.broadcast_to(wgt_t[pl.ds(pl.multiple_of(me * C + h * CH, 8), CH), 0:1], (CH, LANES)), FD
        )
        for b in range(PR // RB):
            rows = slice(b * RB, (b + 1) * RB)
            vals = [frecv[h, j, rows, :].astype(F32) for j in range(M)]
            total = [None] * M
            for a in range(M):
                for c in range(a + 1, M):
                    k = smooth(vals[a] - vals[c])
                    total[a] = k if total[a] is None else total[a] + k
                    total[c] = -k if total[c] is None else total[c] - k
            for a in range(M):
                g = wp[rows] * (smooth(vals[a] - tp[rows]) - total[a] * (1.0 / M))
                gsend[h, a, rows, :] = g.astype(BF)
        for k in range(HM):
            g_copy(h, far + k, 0).start()
        for k in range(1, HM):
            g_copy(h, same_half(k), 1).start()
        gf[h, me] = gsend[h, me]
        for b in range(K // LANES):
            rel, at = b * LANES // B, b * LANES % B
            cols = slice(LANES * b, LANES * b + LANES)
            lat_t[h, :, cols] = lat[rel * PH + h].reshape(B, D)[at : at + LANES, :].T
            hid_t[h, :, cols] = hid[pl.ds(pl.multiple_of((rel * PH + h) * B + at, LANES), LANES), :].T
        return carry

    with jax.named_scope("pairs"):
        lax.fori_loop(0, PH, phase, 0)

    def back(h, rel):
        blk = 2 * h + rel
        for k in range(HM):
            p = gf[h, (near if rel else far) + k]
            at = pl.multiple_of(blk * B + k * CH, CH)
            gfu[pl.ds(at, PR), :] = p
            gfu[pl.ds(pl.multiple_of(at + PR, CH - PR), CH - PR), :] = unpack_last(p.astype(F32), FD).astype(BF)
        rows = pl.ds(pl.multiple_of(blk * B, B), B)
        held = pl.ds(pl.multiple_of((rel * PH + h) * B, B), B)
        gp[rows, :] = (mm(gfu[rows, :], wh[...]) * slope[held, :]).astype(BF)

    def gather(h):
        arrived(gf.at[h, pl.ds(0, HM - 1)], sem_gr.at[1, h])
        back(h, 1)
        arrived(gf.at[h, pl.ds(0, HM)], sem_gr.at[0, h])
        back(h, 0)

    def terms(h, p):
        rows = pl.ds(pl.multiple_of(p * (2 * r * CN), 2 * r * CN), 2 * r * CN)
        at = pl.ds(pl.multiple_of(h * K, K), K)
        return mm(lat_t[h, rows, :], gp[at, :]), mm(hid_t[h, rows, :], gfu[at, :])

    def early(h, carry):
        gather(h)

        def add(p, c):
            a, b = terms(h, p)

            @pl.when(h == 0)
            def _():
                acc[p, :, :H] = a
                acc[p, :, H:] = b

            @pl.when(h > 0)
            def _():
                acc[p, :, :H] += a
                acc[p, :, H:] += b

            return c

        return lax.fori_loop(0, PB, add, carry)

    with jax.named_scope("early"):
        lax.fori_loop(0, PH - 1, early, 0)

    with jax.named_scope("gather"):
        gather(PH - 1)

    def first(i):
        p = block_of(i)
        a, b = terms(PH - 1, p)
        v = jnp.concatenate([a + acc[p, :, :H], b + acc[p, :, H:]], axis=1)
        for s in range(2):
            for g in range(G):
                at = (s * CN + 2 * g) * r
                low, high = v[at : at + r], v[at + r : at + 2 * r]
                sb[i, s, g] = jnp.where(core == 0, high, low).astype(BF)
                kf[i, s, g] = jnp.where(core == 0, low, high)
        c1(i).start()

    def start_second(i, q):
        for d in range(1, G):
            c2a(i, q, d).start()
        c2b(i, q).start()

    def second(i):
        c1(i).wait_recv()
        for s in range(2):
            for g in range(G):
                v = kf[i, s, g] + r1[i, s, g].astype(F32)
                kf[i, s, g] = v
                s2[i, s, g] = v.astype(BF)

        @pl.when(i < 2)
        def _():
            for q in range(NQ):
                start_second(i, q)

    NQ = len(chunks)

    def opening(i, carry):
        @pl.when(i < PB)
        def _():
            first(i)

        @pl.when(i >= 2)
        def _():
            second(i - 2)

        return carry

    with jax.named_scope("opening"):
        lax.fori_loop(0, PB + 2, opening, 0)

    def third(i, q):
        a0, a1, b1 = chunks[q]
        for d in range(1, G):
            c2a(i, q, d).wait_recv()
        away = kf[i, 1 - x, grp, :, a0:a1]
        keep = kf[i, x, grp, :, a0:a1]
        for d in range(1, G):
            away = away + r2a[i, d - 1, 1 - x, :, a0:a1].astype(F32)
            keep = keep + r2a[i, d - 1, x, :, a0:a1].astype(F32)
        s3a[i, :, a0:a1] = away.astype(BF)
        c3a(i, q).start()
        k3[i, :, a0:a1] = keep
        c2b(i, q).wait_recv()
        for g in range(G):
            s3b[i, g, :, a1:b1] = (kf[i, x, g, :, a1:b1] + r2b[i, g, :, a1:b1].astype(F32)).astype(BF)
        for d in range(1, G):
            c3b(i, q, d).start()
        k3[i, :, a1:b1] = kf[i, x, grp, :, a1:b1] + r2b[i, grp, :, a1:b1].astype(F32)

        @pl.when(i + 2 < PB)
        def _():
            start_second(i + 2, q)

    def fourth(i, q):
        a0, a1, b1 = chunks[q]
        c3a(i, q).wait_recv()
        u = k3[i, :, a0:a1] + r3a[i, :, a0:a1].astype(F32)
        v = k3[i, :, a1:b1]
        for d in range(1, G):
            c3b(i, q, d).wait_recv()
            v = v + r3b[i, d - 1, :, a1:b1].astype(F32)

        @pl.when(i < PB - 1)
        def _():
            sz[i, :, a0:a1] = u.astype(BF)
            sz[i, :, a1:b1] = v.astype(BF)
            c4(i, q).start()

        @pl.when(i == PB - 1)
        def _():
            k3[i, :, a0:a1] = u
            k3[i, :, a1:b1] = v

    def stages(i, carry):
        for q in range(NQ):
            @pl.when(i >= 2)
            def _():
                fourth(i - 2, q)

            @pl.when(i < PB)
            def _():
                third(i, q)

        return carry

    with jax.named_scope("stages"):
        lax.fori_loop(0, PB + 2, stages, 0)

    with jax.named_scope("last"):
        total = k3[PB - 1]
        arrived(rz.at[pl.ds(0, PB - 1)], sem4r.at[0])
        for i in range(PB - 1):
            total = total + rz[i].astype(F32)
        out_in[...] = total[:, :H]
        out_out[...] = total[:, H : H + FD]

    arrived(fsend.at[:, pl.ds(0, M - 1)], sem_fs.at[0])
    arrived(gsend.at[:, pl.ds(0, M - 1)], sem_gs.at[0])
    arrived(sb, sem1s.at[0])
    wide = pl.ds(0, sum(c[1] - c[0] for c in chunks))
    narrow = pl.ds(0, sum(c[2] - c[1] for c in chunks))
    arrived(s2.at[:, :, pl.ds(0, G - 1), :, wide], sem2as.at[0])
    arrived(s2.at[:, 0, :, :, narrow], sem2bs.at[0])
    arrived(s3a.at[:, :, wide], sem3as.at[0])
    arrived(s3b.at[:, pl.ds(0, G - 1), :, narrow], sem3bs.at[0])
    arrived(sz.at[pl.ds(0, PB - 1)], sem4s.at[0])


def publish(res_in, res_out, out_in, out_out, sem):
    a = pltpu.make_async_copy(res_in, out_in, sem.at[0])
    b = pltpu.make_async_copy(res_out, out_out, sem.at[1])
    a.start()
    b.start()
    a.wait()
    b.wait()


def per_device(latent, w_in, w_out, target, cell_mask):
    M = lax.axis_size("member")
    CN = lax.axis_size("cell")
    N, D = latent.shape[1:]
    H = w_in.shape[1]
    FD = w_out.shape[1]
    PH = PHASES
    C = N // M
    CH = C // PH
    K = M * CH
    PB, G = M // 2, CN // 2
    n = FD // (LANES - FD)
    PR = CH // (n + 1) * n
    r = D // (M * CN)
    W = H + LANES
    T = W // LANES
    chunks, at = [], 0
    for tiles in ((T + 1) // 2, T // 2):
        chunks.append((at * LANES, (at + (tiles + 1) // 2) * LANES, (at + tiles) * LANES))
        at += tiles
    NQ = len(chunks)
    NB = -(-(LANES - math.gcd(C, LANES) + C) // LANES)
    GS = max(G - 1, 1)
    V = pltpu.VMEM
    DMA = pltpu.SemaphoreType.DMA
    vm = pl.BlockSpec(memory_space=pltpu.VMEM)
    res = pl.pallas_call(
        functools.partial(body, M, CN, tuple(chunks)),
        out_shape=(V((r, H), F32), V((r, FD), F32)),
        in_specs=[pl.BlockSpec(memory_space=pl.ANY)] * 5,
        out_specs=(vm, vm),
        scratch_shapes=[
            V((2 * PH, M // 2, CH, D), BF), V((D, H), BF), V((LANES, H), BF), V((LANES, H), BF),
            V((FD, N), BF), V((N,), jnp.int32),
            V((N, H), F32), V((N, H), BF), V((N, H), BF), V((N, LANES), BF), V((PH, D, K), BF), V((PH, H, K), BF),
            V((NB * LANES, LANES), F32), V((N, 8), F32),
            V((PH, M, PR, LANES), BF), V((PH, M, PR, LANES), BF), V((PH, M, PR, LANES), BF), V((PH, M, PR, LANES), BF),
            V((PB, 2 * CN * r, W), F32), V((PB, 2, G, r, W), F32), V((PB, 2, G, r, W), BF), V((PB, 2, G, r, W), BF),
            V((PB, 2, G, r, W), BF), V((PB, GS, 2, r, W), BF), V((PB, G, r, W), BF),
            V((PB, r, W), F32), V((PB, r, W), BF), V((PB, r, W), BF), V((PB, G, r, W), BF), V((PB, GS, r, W), BF),
            V((PB, r, W), BF), V((PB, r, W), BF),
            DMA((2 * PH + 4,)), DMA((1,)), DMA((PH,)), DMA((1,)), DMA((2, PH)),
            DMA((1,)), DMA((PB,)), DMA((1,)), DMA((NQ, PB, GS)), DMA((1,)), DMA((NQ, PB)),
            DMA((1,)), DMA((NQ, PB)), DMA((1,)), DMA((NQ, PB, GS)), DMA((1,)), DMA((1,)),
        ],
        compiler_params=pltpu.CompilerParams(
            collective_id=0, has_side_effects=True, vmem_limit_bytes=60 * 1024 * 1024
        ),
    )(latent.reshape(M, C, D), w_in, w_out.T, target, cell_mask)
    return pl.pallas_call(
        publish,
        out_shape=(jax.ShapeDtypeStruct((r, H), F32), jax.ShapeDtypeStruct((r, FD), F32)),
        in_specs=[vm, vm],
        out_specs=(pl.BlockSpec(memory_space=pl.ANY),) * 2,
        scratch_shapes=[DMA((2,))],
        compiler_params=pltpu.CompilerParams(vmem_limit_bytes=1024 * 1024),
    )(*(pltpu.with_memory_space_constraint(o, pltpu.VMEM) for o in res))


def solution(mesh):
    in_specs = (P("member", "cell", None), P(), P(), P(None, "cell"), P("cell"))
    out_specs = (P(("member", "cell"), None), P(("member", "cell"), None))
    return jax.shard_map(
        per_device, mesh=mesh, in_specs=in_specs, out_specs=out_specs, check_vma=False
    )
```

time: 51.6 us -> 45.1 us (0.87)
  Pallas kernels: 50.8 us -> 44.3 us
    pallas_call x2, Pallas kernels: 50.8 us -> 44.3 us  [the longest x1 43.7 us: per_device(): pl.pallas_call(functools.partial(body, M, CN, tuple(chunks)), out_shape=(...]
where the time goes in v2:
time: 45.1 us; the launch traced here: 45 us
  Pallas kernels  44.3 us (98%)
  between operations  0.64 us (1%)
    pallas_call x1, Pallas kernels, per_device(): pl.pallas_call(functools.partial(body, M, CN, tuple(chunks)), out_shape=(...  43.7 us

profile of v2, /device:TPU:0, one launch (start us, length us, event | category | flops | bytes accessed | tf_op | source)
XLA Modules:
  0.0 45.0 jit_solution(6329326431937752868)
XLA Ops:
  0.6 43.7 %shard_map.68 = (f32[32,1024]{1,0:T(8,128)S(1)}, f32[32,96]{1,0:T(8,128)S(1)}) custom-call(bf16[8,192,1024]{2,1,0:T(8,128)(2,1)} %bitcast.2, bf16[1024,1024]{1,0:T(8,128)(2,1)} %w_in_hbm.1, bf16[96,1024]{1,0:T(8,128)(2,1)} %bitcast.3, bf16[96,1536]{1,0:T(8,128)(2,1)} %target_hbm.1, s32[1536]{0:T(1024)} %mask_hbm.1), custom_call_target="tpu_custom_call" | custom-call | tf_op jit(solution)/shard_map/pallas_call | solution.py:475
  44.3 0.7 %shard_map.69 = (f32[32,1024]{1,0:T(8,128)}, f32[32,96]{1,0:T(8,128)}) custom-call(f32[32,1024]{1,0:T(8,128)S(1)} %get-tuple-element.4.res_in, f32[32,96]{1,0:T(8,128)S(1)} %get-tuple-element.5.res_out), custom_call_target="tpu_custom_call" | custom-call | tf_op jit(solution)/shard_map/pallas_call | solution.py:498

commit v3 on v2

--- a/solution.py
+++ b/solution.py
@@ -101,13 +101,13 @@
     load_o = pltpu.make_async_copy(w_out_hbm, wo.at[pl.ds(0, FD), :], sem_in.at[2 * PH + 1])
     load_t = pltpu.make_async_copy(target_hbm, target, sem_in.at[2 * PH + 2])
     load_m = pltpu.make_async_copy(mask_hbm, mask, sem_in.at[2 * PH + 3])
+    load_t.start()
+    load_m.start()
     load_w.start()
     load(0, 0).start()
     load_o.start()
     for i in range(1, 2 * PH):
-        load(i // PH, i % PH).start()
-    load_t.start()
-    load_m.start()
+        load(i % 2, i // 2).start()
     wo[FD:, :] = jnp.zeros((LANES - FD, H), BF)
 
     def f_copy(h, t):
@@ -178,12 +178,11 @@
             device_id=(block_of(i) * 2 + x, cell), device_id_type=MESH,
         )
 
-    def decode(rel, h0, blocks):
-        at = rel * PH + h0
-        rows = slice(at * B, (at + blocks) * B)
-        for h in range(h0, h0 + blocks):
-            load(rel, h).wait()
-        v = mm(lat[at : at + blocks].reshape(blocks * B, D), w_in[...])
+    def decode(rel, h):
+        at = rel * PH + h
+        rows = slice(at * B, (at + 1) * B)
+        load(rel, h).wait()
+        v = mm(lat[at].reshape(B, D), w_in[...])
         u = 0.5 * v
         t = jnp.tanh(u)
         ut = u * t
@@ -192,33 +191,20 @@
         hid[rows, :] = hb
         return lax.dot_general(hb, wo[...], (((1,), (1,)), ((), ())), preferred_element_type=F32)
 
-    def send_fields(rel, h0, blocks, f):
-        for h in range(h0, h0 + blocks):
-            for k in range(HM):
-                at = ((h - h0) * HM + k) * CH
-                t = (near if rel else far) + k
-                fsend[h, t] = pack(f[at : at + CH], FD).astype(BF)
-                if not rel:
-                    f_copy(h, t).start()
-            if rel:
-                frecv[h, me] = fsend[h, me]
-                for k in range(1, HM):
-                    f_copy(h, same_half(k)).start()
-
-    with jax.named_scope("forward"):
-        load_w.wait()
-        load_o.wait()
-        f = decode(0, 0, 1)
-        pl.semaphore_wait(barrier, M - 1 + 1 + G - 1)
-        send_fields(0, 0, 1, f)
-        send_fields(0, 1, PH - 1, decode(0, 1, PH - 1))
-        send_fields(1, 0, 1, decode(1, 0, 1))
-        send_fields(1, 1, PH - 1, decode(1, 1, PH - 1))
+    def send_fields(rel, h, f):
+        for k in range(HM):
+            t = (near if rel else far) + k
+            fsend[h, t] = pack(f[k * CH : (k + 1) * CH], FD).astype(BF)
+            if not rel:
+                f_copy(h, t).start()
+        if rel:
+            frecv[h, me] = fsend[h, me]
+            for k in range(1, HM):
+                f_copy(h, same_half(k)).start()
 
     with jax.named_scope("prep"):
         load_t.wait()
         load_m.wait()
-        wh[...] = (0.5 * wo[...].astype(F32)).astype(BF)
         NB = tgt_t.shape[0] // LANES
         b0 = jnp.minimum(me * C // LANES, N // LANES - NB)
         for b in range(NB):
@@ -228,6 +214,16 @@
             cols = slice(LANES * b, LANES * b + LANES)
             w = mask[cols].astype(F32) * scale
             wgt_t[cols, :] = jnp.broadcast_to(w[None, :], (8, LANES)).T
+
+    with jax.named_scope("forward"):
+        load_w.wait()
+        load_o.wait()
+        f = decode(0, 0)
+        pl.semaphore_wait(barrier, M - 1 + 1 + G - 1)
+        send_fields(0, 0, f)
+        for i in range(1, 2 * PH):
+            send_fields(i % 2, i // 2, decode(i % 2, i // 2))
+        wh[...] = (0.5 * wo[...].astype(F32)).astype(BF)
 
     RB = 16 if PR % 16 == 0 else PR
 
@@ -257,9 +253,9 @@
         gf[h, me] = gsend[h, me]
         for b in range(K // LANES):
             rel, at = b * LANES // B, b * LANES % B
-            cols = slice(LANES * b, LANES * b + LANES)
-            lat_t[h, :, cols] = lat[rel * PH + h].reshape(B, D)[at : at + LANES, :].T
-            hid_t[h, :, cols] = hid[pl.ds(pl.multiple_of((rel * PH + h) * B + at, LANES), LANES), :].T
+            cols = pl.ds(pl.multiple_of(h * K + LANES * b, LANES), LANES)
+            lat_t[:, cols] = lat[rel * PH + h].reshape(B, D)[at : at + LANES, :].T
+            hid_t[:, cols] = hid[pl.ds(pl.multiple_of((rel * PH + h) * B + at, LANES), LANES), :].T
         return carry
 
     with jax.named_scope("pairs"):
@@ -282,41 +278,27 @@
         arrived(gf.at[h, pl.ds(0, HM)], sem_gr.at[0, h])
         back(h, 0)
 
-    def terms(h, p):
-        rows = pl.ds(pl.multiple_of(p * (2 * r * CN), 2 * r * CN), 2 * r * CN)
-        at = pl.ds(pl.multiple_of(h * K, K), K)
-        return mm(lat_t[h, rows, :], gp[at, :]), mm(hid_t[h, rows, :], gfu[at, :])
-
-    def early(h, carry):
-        gather(h)
-
-        def add(p, c):
-            a, b = terms(h, p)
-
-            @pl.when(h == 0)
-            def _():
-                acc[p, :, :H] = a
-                acc[p, :, H:] = b
-
-            @pl.when(h > 0)
-            def _():
-                acc[p, :, :H] += a
-                acc[p, :, H:] += b
-
-            return c
-
-        return lax.fori_loop(0, PB, add, carry)
+    def terms(h0, phases, i):
+        rows = pl.ds(pl.multiple_of(block_of(i) * (2 * r * CN), 2 * r * CN), 2 * r * CN)
+        at = slice(h0 * K, (h0 + phases) * K)
+        return jnp.concatenate([mm(lat_t[rows, at], gp[at, :]), mm(hid_t[rows, at], gfu[at, :])], axis=1)
+
+    def early(i, carry):
+        acc[i] = terms(0, 1, i)
+        return carry
 
     with jax.named_scope("early"):
-        lax.fori_loop(0, PH - 1, early, 0)
+        gather(0)
+        lax.fori_loop(0, PB, early, 0)
+        for h in range(1, PH - 1):
+            gather(h)
+        acc[0] += terms(1, PH - 2, 0)
 
     with jax.named_scope("gather"):
         gather(PH - 1)
 
-    def first(i):
-        p = block_of(i)
-        a, b = terms(PH - 1, p)
-        v = jnp.concatenate([a + acc[p, :, :H], b + acc[p, :, H:]], axis=1)
+    def first(i, v):
+        v = v + acc[i]
         for s in range(2):
             for g in range(G):
                 at = (s * CN + 2 * g) * r
@@ -338,26 +320,22 @@
                 kf[i, s, g] = v
                 s2[i, s, g] = v.astype(BF)
 
-        @pl.when(i < 2)
-        def _():
-            for q in range(NQ):
+        for q in range(2):
+            @pl.when(2 * i + q < 5)
+            def _():
                 start_second(i, q)
-
-    NQ = len(chunks)
 
     def opening(i, carry):
         @pl.when(i < PB)
         def _():
-            first(i)
-
-        @pl.when(i >= 2)
-        def _():
-            second(i - 2)
-
+            first(i, terms(1, PH - 1, i))
+
+        second(i - 1)
         return carry
 
     with jax.named_scope("opening"):
-        lax.fori_loop(0, PB + 2, opening, 0)
+        first(0, terms(PH - 1, 1, 0))
+        lax.fori_loop(1, PB + 1, opening, 0)
 
     def third(i, q):
         a0, a1, b1 = chunks[q]
@@ -378,9 +356,11 @@
             c3b(i, q, d).start()
         k3[i, :, a1:b1] = kf[i, x, grp, :, a1:b1] + r2b[i, grp, :, a1:b1].astype(F32)
 
-        @pl.when(i + 2 < PB)
+        ahead = i + (5 + q) // 2
+
+        @pl.when(ahead < PB)
         def _():
-            start_second(i + 2, q)
+            start_second(ahead, (5 + q) % 2)
 
     def fourth(i, q):
         a0, a1, b1 = chunks[q]
@@ -403,14 +383,14 @@
             k3[i, :, a1:b1] = v
 
     def stages(i, carry):
-        for q in range(NQ):
+        for q in range(2):
+            @pl.when(i < PB)
+            def _():
+                third(i, q)
+
             @pl.when(i >= 2)
             def _():
                 fourth(i - 2, q)
-
-            @pl.when(i < PB)
-            def _():
-                third(i, q)
 
         return carry
 
@@ -480,7 +460,7 @@
         scratch_shapes=[
             V((2 * PH, M // 2, CH, D), BF), V((D, H), BF), V((LANES, H), BF), V((LANES, H), BF),
             V((FD, N), BF), V((N,), jnp.int32),
-            V((N, H), F32), V((N, H), BF), V((N, H), BF), V((N, LANES), BF), V((PH, D, K), BF), V((PH, H, K), BF),
+            V((N, H), F32), V((N, H), BF), V((N, H), BF), V((N, LANES), BF), V((D, N), BF), V((H, N), BF),
             V((NB * LANES, LANES), F32), V((N, 8), F32),
             V((PH, M, PR, LANES), BF), V((PH, M, PR, LANES), BF), V((PH, M, PR, LANES), BF), V((PH, M, PR, LANES), BF),
             V((PB, 2 * CN * r, W), F32), V((PB, 2, G, r, W), F32), V((PB, 2, G, r, W), BF), V((PB, 2, G, r, W), BF),

time: 45.1 us -> 42.7 us (0.947)
  Pallas kernels: 44.3 us -> 41.9 us
    pallas_call x1, Pallas kernels: 43.7 us -> 41.2 us  [per_device(): pl.pallas_call(functools.partial(body, M, CN, tuple(chunks)), out_shape=(...]
where the time goes in v3:
time: 42.7 us; the launch traced here: 42.6 us
  Pallas kernels  41.9 us (98%)
  between operations  0.64 us (1%)
    pallas_call x1, Pallas kernels, per_device(): pl.pallas_call(functools.partial(body, M, CN, tuple(chunks)), out_shape=(...  41.2 us

profile of v3, /device:TPU:0, one launch (start us, length us, event | category | flops | bytes accessed | tf_op | source)
XLA Modules:
  0.0 42.6 jit_solution(7854277017622674557)
XLA Ops:
  0.6 41.2 %shard_map.68 = (f32[32,1024]{1,0:T(8,128)S(1)}, f32[32,96]{1,0:T(8,128)S(1)}) custom-call(bf16[8,192,1024]{2,1,0:T(8,128)(2,1)} %bitcast.2, bf16[1024,1024]{1,0:T(8,128)(2,1)} %w_in_hbm.1, bf16[96,1024]{1,0:T(8,128)(2,1)} %bitcast.3, bf16[96,1536]{1,0:T(8,128)(2,1)} %target_hbm.1, s32[1536]{0:T(1024)} %mask_hbm.1), custom_call_target="tpu_custom_call" | custom-call | tf_op jit(solution)/shard_map/pallas_call | solution.py:455
  41.9 0.7 %shard_map.69 = (f32[32,1024]{1,0:T(8,128)}, f32[32,96]{1,0:T(8,128)}) custom-call(f32[32,1024]{1,0:T(8,128)S(1)} %get-tuple-element.4.res_in, f32[32,96]{1,0:T(8,128)S(1)} %get-tuple-element.5.res_out), custom_call_target="tpu_custom_call" | custom-call | tf_op jit(solution)/shard_map/pallas_call | solution.py:478

commit v4 on v3

--- a/solution.py
+++ b/solution.py
@@ -13,6 +13,8 @@
 F32 = jnp.float32
 LANES = 128
 PHASES = 3
+AHEAD = 4
+BEHIND = 3
 
 
 def smooth(d):
@@ -283,22 +285,22 @@
         at = slice(h0 * K, (h0 + phases) * K)
         return jnp.concatenate([mm(lat_t[rows, at], gp[at, :]), mm(hid_t[rows, at], gfu[at, :])], axis=1)
 
-    def early(i, carry):
-        acc[i] = terms(0, 1, i)
-        return carry
+    early = [PH - 1, 1]
 
     with jax.named_scope("early"):
-        gather(0)
-        lax.fori_loop(0, PB, early, 0)
-        for h in range(1, PH - 1):
+        for h in range(PH - 1):
             gather(h)
-        acc[0] += terms(1, PH - 2, 0)
+            for i, phases in enumerate(early):
+                if h < phases:
+                    if h == 0:
+                        acc[i] = terms(h, 1, i)
+                    else:
+                        acc[i] += terms(h, 1, i)
 
     with jax.named_scope("gather"):
         gather(PH - 1)
 
     def first(i, v):
-        v = v + acc[i]
         for s in range(2):
             for g in range(G):
                 at = (s * CN + 2 * g) * r
@@ -320,22 +322,19 @@
                 kf[i, s, g] = v
                 s2[i, s, g] = v.astype(BF)
 
-        for q in range(2):
-            @pl.when(2 * i + q < 5)
-            def _():
-                start_second(i, q)
-
-    def opening(i, carry):
-        @pl.when(i < PB)
-        def _():
-            first(i, terms(1, PH - 1, i))
-
-        second(i - 1)
-        return carry
+    pieces = [(i, q) for i in range(PB) for q in range(len(chunks))]
 
     with jax.named_scope("opening"):
-        first(0, terms(PH - 1, 1, 0))
-        lax.fori_loop(1, PB + 1, opening, 0)
+        for i in range(PB + 1):
+            if i < PB:
+                known = early[i] if i < len(early) else 0
+                v = terms(known, PH - known, i)
+                first(i, v + acc[i] if known else v)
+            if i >= 1:
+                second(i - 1)
+                for j, q in pieces[:AHEAD]:
+                    if j == i - 1:
+                        start_second(j, q)
 
     def third(i, q):
         a0, a1, b1 = chunks[q]
@@ -356,12 +355,6 @@
             c3b(i, q, d).start()
         k3[i, :, a1:b1] = kf[i, x, grp, :, a1:b1] + r2b[i, grp, :, a1:b1].astype(F32)
 
-        ahead = i + (5 + q) // 2
-
-        @pl.when(ahead < PB)
-        def _():
-            start_second(ahead, (5 + q) % 2)
-
     def fourth(i, q):
         a0, a1, b1 = chunks[q]
         c3a(i, q).wait_recv()
@@ -371,31 +364,22 @@
             c3b(i, q, d).wait_recv()
             v = v + r3b[i, d - 1, :, a1:b1].astype(F32)
 
-        @pl.when(i < PB - 1)
-        def _():
+        if i < PB - 1:
             sz[i, :, a0:a1] = u.astype(BF)
             sz[i, :, a1:b1] = v.astype(BF)
             c4(i, q).start()
-
-        @pl.when(i == PB - 1)
-        def _():
+        else:
             k3[i, :, a0:a1] = u
             k3[i, :, a1:b1] = v
 
-    def stages(i, carry):
-        for q in range(2):
-            @pl.when(i < PB)
-            def _():
-                third(i, q)
-
-            @pl.when(i >= 2)
-            def _():
-                fourth(i - 2, q)
-
-        return carry
-
     with jax.named_scope("stages"):
-        lax.fori_loop(0, PB + 2, stages, 0)
+        for u in range(len(pieces) + BEHIND):
+            if u < len(pieces):
+                third(*pieces[u])
+                if u + AHEAD < len(pieces):
+                    start_second(*pieces[u + AHEAD])
+            if u >= BEHIND:
+                fourth(*pieces[u - BEHIND])
 
     with jax.named_scope("last"):
         total = k3[PB - 1]
@@ -463,7 +447,7 @@
             V((N, H), F32), V((N, H), BF), V((N, H), BF), V((N, LANES), BF), V((D, N), BF), V((H, N), BF),
             V((NB * LANES, LANES), F32), V((N, 8), F32),
             V((PH, M, PR, LANES), BF), V((PH, M, PR, LANES), BF), V((PH, M, PR, LANES), BF), V((PH, M, PR, LANES), BF),
-            V((PB, 2 * CN * r, W), F32), V((PB, 2, G, r, W), F32), V((PB, 2, G, r, W), BF), V((PB, 2, G, r, W), BF),
+            V((2, 2 * CN * r, W), F32), V((PB, 2, G, r, W), F32), V((PB, 2, G, r, W), BF), V((PB, 2, G, r, W), BF),
             V((PB, 2, G, r, W), BF), V((PB, GS, 2, r, W), BF), V((PB, G, r, W), BF),
             V((PB, r, W), F32), V((PB, r, W), BF), V((PB, r, W), BF), V((PB, G, r, W), BF), V((PB, GS, r, W), BF),
             V((PB, r, W), BF), V((PB, r, W), BF),

time: 42.7 us -> 41.1 us (0.963)
  Pallas kernels: 41.9 us -> 40.3 us
    pallas_call x1, Pallas kernels: 41.2 us -> 39.6 us  [per_device(): pl.pallas_call(functools.partial(body, M, CN, tuple(chunks)), out_shape=(...]
where the time goes in v4:
time: 41.1 us; the launch traced here: 40.9 us
  Pallas kernels  40.3 us (98%)
  between operations  0.64 us (2%)
    pallas_call x1, Pallas kernels, per_device(): pl.pallas_call(functools.partial(body, M, CN, tuple(chunks)), out_shape=(...  39.6 us

profile of v4, /device:TPU:0, one launch (start us, length us, event | category | flops | bytes accessed | tf_op | source)
XLA Modules:
  0.0 40.9 jit_solution(4675384524641968941)
XLA Ops:
  0.6 39.6 %shard_map.68 = (f32[32,1024]{1,0:T(8,128)S(1)}, f32[32,96]{1,0:T(8,128)S(1)}) custom-call(bf16[8,192,1024]{2,1,0:T(8,128)(2,1)} %bitcast.2, bf16[1024,1024]{1,0:T(8,128)(2,1)} %w_in_hbm.1, bf16[96,1024]{1,0:T(8,128)(2,1)} %bitcast.3, bf16[96,1536]{1,0:T(8,128)(2,1)} %target_hbm.1, s32[1536]{0:T(1024)} %mask_hbm.1), custom_call_target="tpu_custom_call" | custom-call | tf_op jit(solution)/shard_map/pallas_call | solution.py:439
  40.3 0.7 %shard_map.69 = (f32[32,1024]{1,0:T(8,128)}, f32[32,96]{1,0:T(8,128)}) custom-call(f32[32,1024]{1,0:T(8,128)S(1)} %get-tuple-element.4.res_in, f32[32,96]{1,0:T(8,128)S(1)} %get-tuple-element.5.res_out), custom_call_target="tpu_custom_call" | custom-call | tf_op jit(solution)/shard_map/pallas_call | solution.py:462

commit v5 on v4

--- a/solution.py
+++ b/solution.py
@@ -15,6 +15,8 @@
 PHASES = 3
 AHEAD = 4
 BEHIND = 3
+LATE = 1
+DIRECT = (1, 3, 0)
 
 
 def smooth(d):
@@ -49,13 +51,13 @@
 
 
 def body(
-    M, CN, chunks,
+    M, CN, kinds, chunks,
     lat_hbm, w_in_hbm, w_out_hbm, target_hbm, mask_hbm, out_in, out_out,
     lat, w_in, wo, wh, target, mask, slope, hid, gp, gfu, lat_t, hid_t, tgt_t, wgt_t,
     fsend, frecv, gsend, gf,
-    acc, kf, sb, r1, s2, r2a, r2b, k3, s3a, r3a, s3b, r3b, sz, rz,
+    acc, kf, sb, r1, s2, r2a, r2b, k3, s3a, r3a, s3b, r3b, sz, rz, r5,
     sem_in, sem_fs, sem_fr, sem_gs, sem_gr,
-    sem1s, sem1r, sem2as, sem2ar, sem2bs, sem2br, sem3as, sem3ar, sem3bs, sem3br, sem4s, sem4r,
+    sem1s, sem1r, sem2as, sem2ar, sem2bs, sem2br, sem3as, sem3ar, sem3bs, sem3br, sem4s, sem4r, sem5s, sem5r,
 ):
     me = lax.axis_index("member")
     cell = lax.axis_index("cell")
@@ -136,32 +138,32 @@
         )
 
     def c2a(i, q, d):
-        cols = pl.ds(chunks[q][0], chunks[q][1] - chunks[q][0])
+        cols = pl.ds(chunks[kinds[i]][q][0], chunks[kinds[i]][q][1] - chunks[kinds[i]][q][0])
         g = lax.rem(grp + d, G)
         return pltpu.make_async_remote_copy(
-            s2.at[i, :, g, :, cols], r2a.at[i, d - 1, :, :, cols], sem2as.at[0], sem2ar.at[q, i, d - 1],
+            s2.at[i, :, g, :, cols], r2a.at[i, d - 1, :, :, cols], sem2as.at[kinds[i]], sem2ar.at[q, i, d - 1],
             device_id=(me, g * 2 + core), device_id_type=MESH,
         )
 
     def c2b(i, q):
-        cols = pl.ds(chunks[q][1], chunks[q][2] - chunks[q][1])
-        return pltpu.make_async_remote_copy(
-            s2.at[i, 1 - x, :, :, cols], r2b.at[i, :, :, cols], sem2bs.at[0], sem2br.at[q, i],
+        cols = pl.ds(chunks[kinds[i]][q][1], chunks[kinds[i]][q][2] - chunks[kinds[i]][q][1])
+        return pltpu.make_async_remote_copy(
+            s2.at[i, 1 - x, :, :, cols], r2b.at[i, :, :, cols], sem2bs.at[kinds[i]], sem2br.at[q, i],
             device_id=pair_x, device_id_type=MESH,
         )
 
     def c3a(i, q):
-        cols = pl.ds(chunks[q][0], chunks[q][1] - chunks[q][0])
-        return pltpu.make_async_remote_copy(
-            s3a.at[i, :, cols], r3a.at[i, :, cols], sem3as.at[0], sem3ar.at[q, i],
+        cols = pl.ds(chunks[kinds[i]][q][0], chunks[kinds[i]][q][1] - chunks[kinds[i]][q][0])
+        return pltpu.make_async_remote_copy(
+            s3a.at[i, :, cols], r3a.at[i, :, cols], sem3as.at[kinds[i]], sem3ar.at[q, i],
             device_id=pair_x, device_id_type=MESH,
         )
 
     def c3b(i, q, d):
-        cols = pl.ds(chunks[q][1], chunks[q][2] - chunks[q][1])
+        cols = pl.ds(chunks[kinds[i]][q][1], chunks[kinds[i]][q][2] - chunks[kinds[i]][q][1])
         g = lax.rem(grp + d, G)
         return pltpu.make_async_remote_copy(
-            s3b.at[i, g, :, cols], r3b.at[i, d - 1, :, cols], sem3bs.at[0], sem3br.at[q, i, d - 1],
+            s3b.at[i, g, :, cols], r3b.at[i, d - 1, :, cols], sem3bs.at[kinds[i]], sem3br.at[q, i, d - 1],
             device_id=(me, g * 2 + core), device_id_type=MESH,
         )
 
@@ -169,14 +171,21 @@
     zh = z // HP
 
     def block_of(i):
-        far = (1 - zh) * HP + lax.rem(z + i + 1, HP)
-        near = zh * HP + lax.rem(z + i + 1, HP)
-        return jnp.where(i < HP, far, near)
+        side = (1 - zh) if i < HP else zh
+        return side * HP + lax.rem(z + i + 1, HP)
 
     def c4(i, q):
-        cols = pl.ds(chunks[q][0], chunks[q][2] - chunks[q][0])
-        return pltpu.make_async_remote_copy(
-            sz.at[i, :, cols], rz.at[i, :, cols], sem4s.at[0], sem4r.at[0],
+        cols = pl.ds(chunks[kinds[i]][q][0], chunks[kinds[i]][q][2] - chunks[kinds[i]][q][0])
+        return pltpu.make_async_remote_copy(
+            sz.at[i, :, cols], rz.at[i, :, cols], sem4s.at[kinds[i]], sem4r.at[kinds[i]],
+            device_id=(block_of(i) * 2 + x, cell), device_id_type=MESH,
+        )
+
+    def c5(i):
+        at = chunks[kinds[i]][-1][2]
+        cols = pl.ds(at, W - at)
+        return pltpu.make_async_remote_copy(
+            s2.at[i, :, :, :, cols], r5.at[i, :, :, :, cols], sem5s.at[i], sem5r.at[i],
             device_id=(block_of(i) * 2 + x, cell), device_id_type=MESH,
         )
 
@@ -321,8 +330,10 @@
                 v = kf[i, s, g] + r1[i, s, g].astype(F32)
                 kf[i, s, g] = v
                 s2[i, s, g] = v.astype(BF)
-
-    pieces = [(i, q) for i in range(PB) for q in range(len(chunks))]
+        if i < PB - 1:
+            c5(i).start()
+
+    pieces = [(i, q) for i in range(PB) for q in range(2)]
 
     with jax.named_scope("opening"):
         for i in range(PB + 1):
@@ -330,14 +341,22 @@
                 known = early[i] if i < len(early) else 0
                 v = terms(known, PH - known, i)
                 first(i, v + acc[i] if known else v)
-            if i >= 1:
+            if 1 <= i < PB:
                 second(i - 1)
                 for j, q in pieces[:AHEAD]:
                     if j == i - 1:
                         start_second(j, q)
 
+    def merge():
+        for i in range(PB - 1):
+            at = chunks[kinds[i]][-1][2]
+            c5(i).wait_recv()
+            kf[PB - 1, :, :, :, at:] += r5[i, :, :, :, at:].astype(F32)
+        at = min(chunks[k][-1][2] for k in kinds)
+        s2[PB - 1, :, :, :, at:] = kf[PB - 1, :, :, :, at:].astype(BF)
+
     def third(i, q):
-        a0, a1, b1 = chunks[q]
+        a0, a1, b1 = chunks[kinds[i]][q]
         for d in range(1, G):
             c2a(i, q, d).wait_recv()
         away = kf[i, 1 - x, grp, :, a0:a1]
@@ -356,7 +375,7 @@
         k3[i, :, a1:b1] = kf[i, x, grp, :, a1:b1] + r2b[i, grp, :, a1:b1].astype(F32)
 
     def fourth(i, q):
-        a0, a1, b1 = chunks[q]
+        a0, a1, b1 = chunks[kinds[i]][q]
         c3a(i, q).wait_recv()
         u = k3[i, :, a0:a1] + r3a[i, :, a0:a1].astype(F32)
         v = k3[i, :, a1:b1]
@@ -376,29 +395,46 @@
         for u in range(len(pieces) + BEHIND):
             if u < len(pieces):
                 third(*pieces[u])
+                if u == LATE:
+                    second(PB - 1)
+                if pieces[min(u + AHEAD, len(pieces) - 1)] == (PB - 1, 1) and u + AHEAD < len(pieces):
+                    merge()
                 if u + AHEAD < len(pieces):
                     start_second(*pieces[u + AHEAD])
             if u >= BEHIND:
                 fourth(*pieces[u - BEHIND])
 
     with jax.named_scope("last"):
+        for k in range(2):
+            mine = [i for i in range(PB - 1) if kinds[i] == k]
+            if mine:
+                cols = slice(0, chunks[k][-1][2])
+                arrived(rz.at[pl.ds(mine[0], len(mine)), :, cols], sem4r.at[k])
+                part = k3[PB - 1, :, cols]
+                for i in mine:
+                    part = part + rz[i, :, cols].astype(F32)
+                k3[PB - 1, :, cols] = part
         total = k3[PB - 1]
-        arrived(rz.at[pl.ds(0, PB - 1)], sem4r.at[0])
-        for i in range(PB - 1):
-            total = total + rz[i].astype(F32)
         out_in[...] = total[:, :H]
         out_out[...] = total[:, H : H + FD]
 
     arrived(fsend.at[:, pl.ds(0, M - 1)], sem_fs.at[0])
     arrived(gsend.at[:, pl.ds(0, M - 1)], sem_gs.at[0])
     arrived(sb, sem1s.at[0])
-    wide = pl.ds(0, sum(c[1] - c[0] for c in chunks))
-    narrow = pl.ds(0, sum(c[2] - c[1] for c in chunks))
-    arrived(s2.at[:, :, pl.ds(0, G - 1), :, wide], sem2as.at[0])
-    arrived(s2.at[:, 0, :, :, narrow], sem2bs.at[0])
-    arrived(s3a.at[:, :, wide], sem3as.at[0])
-    arrived(s3b.at[:, pl.ds(0, G - 1), :, narrow], sem3bs.at[0])
-    arrived(sz.at[pl.ds(0, PB - 1)], sem4s.at[0])
+    for k in range(3):
+        mine = [i for i in range(PB) if kinds[i] == k]
+        if mine:
+            at = pl.ds(mine[0], len(mine))
+            wide = pl.ds(0, sum(c[1] - c[0] for c in chunks[k]))
+            narrow = pl.ds(0, sum(c[2] - c[1] for c in chunks[k]))
+            arrived(s2.at[at, :, pl.ds(0, G - 1), :, wide], sem2as.at[k])
+            arrived(s2.at[at, 0, :, :, narrow], sem2bs.at[k])
+            arrived(s3a.at[at, :, wide], sem3as.at[k])
+            arrived(s3b.at[at, pl.ds(0, G - 1), :, narrow], sem3bs.at[k])
+            if k < 2:
+                arrived(sz.at[at, :, pl.ds(0, chunks[k][-1][2])], sem4s.at[k])
+    for i in range(PB - 1):
+        c5(i).wait_send()
 
 
 def publish(res_in, res_out, out_in, out_out, sem):
@@ -426,18 +462,22 @@
     r = D // (M * CN)
     W = H + LANES
     T = W // LANES
-    chunks, at = [], 0
-    for tiles in ((T + 1) // 2, T // 2):
-        chunks.append((at * LANES, (at + (tiles + 1) // 2) * LANES, (at + tiles) * LANES))
-        at += tiles
-    NQ = len(chunks)
+    chunks = []
+    for direct in DIRECT:
+        tiles, at, cuts = T - direct, 0, []
+        for n, a in (((tiles + 1) // 2, 1), (tiles // 2, tiles % 2)):
+            cuts.append((at * LANES, (at + (n + a) // 2) * LANES, (at + n) * LANES))
+            at += n
+        chunks.append(tuple(cuts))
+    kinds = tuple(0 if i < PB // 2 else 1 if i < PB - 1 else 2 for i in range(PB))
+    NQ = 2
     NB = -(-(LANES - math.gcd(C, LANES) + C) // LANES)
     GS = max(G - 1, 1)
     V = pltpu.VMEM
     DMA = pltpu.SemaphoreType.DMA
     vm = pl.BlockSpec(memory_space=pltpu.VMEM)
     res = pl.pallas_call(
-        functools.partial(body, M, CN, tuple(chunks)),
+        functools.partial(body, M, CN, kinds, tuple(chunks)),
         out_shape=(V((r, H), F32), V((r, FD), F32)),
         in_specs=[pl.BlockSpec(memory_space=pl.ANY)] * 5,
         out_specs=(vm, vm),
@@ -450,10 +490,10 @@
             V((2, 2 * CN * r, W), F32), V((PB, 2, G, r, W), F32), V((PB, 2, G, r, W), BF), V((PB, 2, G, r, W), BF),
             V((PB, 2, G, r, W), BF), V((PB, GS, 2, r, W), BF), V((PB, G, r, W), BF),
             V((PB, r, W), F32), V((PB, r, W), BF), V((PB, r, W), BF), V((PB, G, r, W), BF), V((PB, GS, r, W), BF),
-            V((PB, r, W), BF), V((PB, r, W), BF),
+            V((PB, r, W), BF), V((PB, r, W), BF), V((PB - 1, 2, G, r, W), BF),
             DMA((2 * PH + 4,)), DMA((1,)), DMA((PH,)), DMA((1,)), DMA((2, PH)),
-            DMA((1,)), DMA((PB,)), DMA((1,)), DMA((NQ, PB, GS)), DMA((1,)), DMA((NQ, PB)),
-            DMA((1,)), DMA((NQ, PB)), DMA((1,)), DMA((NQ, PB, GS)), DMA((1,)), DMA((1,)),
+            DMA((1,)), DMA((PB,)), DMA((3,)), DMA((NQ, PB, GS)), DMA((3,)), DMA((NQ, PB)),
+            DMA((3,)), DMA((NQ, PB)), DMA((3,)), DMA((NQ, PB, GS)), DMA((2,)), DMA((2,)), DMA((PB - 1,)), DMA((PB - 1,)),
         ],
         compiler_params=pltpu.CompilerParams(
             collective_id=0, has_side_effects=True, vmem_limit_bytes=60 * 1024 * 1024

time: 41.1 us -> 40.1 us (0.976)
  Pallas kernels: 40.3 us -> 39.3 us
    pallas_call x1, Pallas kernels: 39.6 us -> 38.7 us  [per_device(): pl.pallas_call(functools.partial(body, M, CN, kinds, tuple(chunks)), out_...]
where the time goes in v5:
time: 40.1 us; the launch traced here: 40 us
  Pallas kernels  39.3 us (98%)
  between operations  0.64 us (2%)
    pallas_call x1, Pallas kernels, per_device(): pl.pallas_call(functools.partial(body, M, CN, kinds, tuple(chunks)), out_...  38.7 us

profile of v5, /device:TPU:0, one launch (start us, length us, event | category | flops | bytes accessed | tf_op | source)
XLA Modules:
  0.0 40.0 jit_solution(13135293478132644077)
XLA Ops:
  0.6 38.7 %shard_map.68 = (f32[32,1024]{1,0:T(8,128)S(1)}, f32[32,96]{1,0:T(8,128)S(1)}) custom-call(bf16[8,192,1024]{2,1,0:T(8,128)(2,1)} %bitcast.2, bf16[1024,1024]{1,0:T(8,128)(2,1)} %w_in_hbm.1, bf16[96,1024]{1,0:T(8,128)(2,1)} %bitcast.3, bf16[96,1536]{1,0:T(8,128)(2,1)} %target_hbm.1, s32[1536]{0:T(1024)} %mask_hbm.1), custom_call_target="tpu_custom_call" | custom-call | tf_op jit(solution)/shard_map/pallas_call | solution.py:479
  39.3 0.7 %shard_map.69 = (f32[32,1024]{1,0:T(8,128)}, f32[32,96]{1,0:T(8,128)}) custom-call(f32[32,1024]{1,0:T(8,128)S(1)} %get-tuple-element.4.res_in, f32[32,96]{1,0:T(8,128)S(1)} %get-tuple-element.5.res_out), custom_call_target="tpu_custom_call" | custom-call | tf_op jit(solution)/shard_map/pallas_call | solution.py:502

commit v6 on v5

--- a/solution.py
+++ b/solution.py
@@ -16,7 +16,8 @@
 AHEAD = 4
 BEHIND = 3
 LATE = 1
-DIRECT = (1, 3, 0)
+JOIN = 4
+DIRECT = (1,3,0)
 
 
 def smooth(d):
@@ -397,12 +398,13 @@
                 third(*pieces[u])
                 if u == LATE:
                     second(PB - 1)
-                if pieces[min(u + AHEAD, len(pieces) - 1)] == (PB - 1, 1) and u + AHEAD < len(pieces):
-                    merge()
-                if u + AHEAD < len(pieces):
+                if u + AHEAD < len(pieces) - 1:
                     start_second(*pieces[u + AHEAD])
             if u >= BEHIND:
                 fourth(*pieces[u - BEHIND])
+            if u == len(pieces) - JOIN:
+                merge()
+                start_second(*pieces[-1])
 
     with jax.named_scope("last"):
         for k in range(2):

time: 40.1 us -> 39.6 us (0.988)
    pallas_call x1, Pallas kernels: 38.7 us -> 38.2 us  [per_device(): pl.pallas_call(functools.partial(body, M, CN, kinds, tuple(chunks)), out_...]
where the time goes in v6:
time: 39.6 us; the launch traced here: 39.5 us
  Pallas kernels  38.9 us (98%)
  between operations  0.64 us (2%)
    pallas_call x1, Pallas kernels, per_device(): pl.pallas_call(functools.partial(body, M, CN, kinds, tuple(chunks)), out_...  38.2 us

profile of v6, /device:TPU:0, one launch (start us, length us, event | category | flops | bytes accessed | tf_op | source)
XLA Modules:
  0.0 39.5 jit_solution(11835928736691395527)
XLA Ops:
  0.6 38.2 %shard_map.68 = (f32[32,1024]{1,0:T(8,128)S(1)}, f32[32,96]{1,0:T(8,128)S(1)}) custom-call(bf16[8,192,1024]{2,1,0:T(8,128)(2,1)} %bitcast.2, bf16[1024,1024]{1,0:T(8,128)(2,1)} %w_in_hbm.1, bf16[96,1024]{1,0:T(8,128)(2,1)} %bitcast.3, bf16[96,1536]{1,0:T(8,128)(2,1)} %target_hbm.1, s32[1536]{0:T(1024)} %mask_hbm.1), custom_call_target="tpu_custom_call" | custom-call | tf_op jit(solution)/shard_map/pallas_call | solution.py:481
  38.8 0.7 %shard_map.69 = (f32[32,1024]{1,0:T(8,128)}, f32[32,96]{1,0:T(8,128)}) custom-call(f32[32,1024]{1,0:T(8,128)S(1)} %get-tuple-element.4.res_in, f32[32,96]{1,0:T(8,128)S(1)} %get-tuple-element.5.res_out), custom_call_target="tpu_custom_call" | custom-call | tf_op jit(solution)/shard_map/pallas_call | solution.py:504

commit v7 on v6

--- a/solution.py
+++ b/solution.py
@@ -406,6 +406,22 @@
                 merge()
                 start_second(*pieces[-1])
 
+    arrived(fsend.at[:, pl.ds(0, M - 1)], sem_fs.at[0])
+    arrived(gsend.at[:, pl.ds(0, M - 1)], sem_gs.at[0])
+    arrived(sb, sem1s.at[0])
+    for k in range(3):
+        mine = [i for i in range(PB) if kinds[i] == k]
+        if mine:
+            at = pl.ds(mine[0], len(mine))
+            wide = pl.ds(0, sum(c[1] - c[0] for c in chunks[k]))
+            narrow = pl.ds(0, sum(c[2] - c[1] for c in chunks[k]))
+            arrived(s2.at[at, :, pl.ds(0, G - 1), :, wide], sem2as.at[k])
+            arrived(s2.at[at, 0, :, :, narrow], sem2bs.at[k])
+            arrived(s3a.at[at, :, wide], sem3as.at[k])
+            arrived(s3b.at[at, pl.ds(0, G - 1), :, narrow], sem3bs.at[k])
+    for i in range(PB - 1):
+        c5(i).wait_send()
+
     with jax.named_scope("last"):
         for k in range(2):
             mine = [i for i in range(PB - 1) if kinds[i] == k]
@@ -420,23 +436,10 @@
         out_in[...] = total[:, :H]
         out_out[...] = total[:, H : H + FD]
 
-    arrived(fsend.at[:, pl.ds(0, M - 1)], sem_fs.at[0])
-    arrived(gsend.at[:, pl.ds(0, M - 1)], sem_gs.at[0])
-    arrived(sb, sem1s.at[0])
-    for k in range(3):
+    for k in range(2):
         mine = [i for i in range(PB) if kinds[i] == k]
         if mine:
-            at = pl.ds(mine[0], len(mine))
-            wide = pl.ds(0, sum(c[1] - c[0] for c in chunks[k]))
-            narrow = pl.ds(0, sum(c[2] - c[1] for c in chunks[k]))
-            arrived(s2.at[at, :, pl.ds(0, G - 1), :, wide], sem2as.at[k])
-            arrived(s2.at[at, 0, :, :, narrow], sem2bs.at[k])
-            arrived(s3a.at[at, :, wide], sem3as.at[k])
-            arrived(s3b.at[at, pl.ds(0, G - 1), :, narrow], sem3bs.at[k])
-            if k < 2:
-                arrived(sz.at[at, :, pl.ds(0, chunks[k][-1][2])], sem4s.at[k])
-    for i in range(PB - 1):
-        c5(i).wait_send()
+            arrived(sz.at[pl.ds(mine[0], len(mine)), :, pl.ds(0, chunks[k][-1][2])], sem4s.at[k])
 
 
 def publish(res_in, res_out, out_in, out_out, sem):

time: 39.6 us -> 39.6 us (level)
  no operation moved by 1% of the time
where the time goes in v7:
time: 39.6 us; the launch traced here: 39.5 us
  Pallas kernels  38.8 us (98%)
  between operations  0.64 us (2%)
    pallas_call x1, Pallas kernels, per_device(): pl.pallas_call(functools.partial(body, M, CN, kinds, tuple(chunks)), out_...  38.2 us

profile of v7, /device:TPU:0, one launch (start us, length us, event | category | flops | bytes accessed | tf_op | source)
XLA Modules:
  0.0 39.5 jit_solution(1273636984316429540)
XLA Ops:
  0.6 38.2 %shard_map.68 = (f32[32,1024]{1,0:T(8,128)S(1)}, f32[32,96]{1,0:T(8,128)S(1)}) custom-call(bf16[8,192,1024]{2,1,0:T(8,128)(2,1)} %bitcast.2, bf16[1024,1024]{1,0:T(8,128)(2,1)} %w_in_hbm.1, bf16[96,1024]{1,0:T(8,128)(2,1)} %bitcast.3, bf16[96,1536]{1,0:T(8,128)(2,1)} %target_hbm.1, s32[1536]{0:T(1024)} %mask_hbm.1), custom_call_target="tpu_custom_call" | custom-call | tf_op jit(solution)/shard_map/pallas_call | solution.py:484
  38.8 0.7 %shard_map.69 = (f32[32,1024]{1,0:T(8,128)}, f32[32,96]{1,0:T(8,128)}) custom-call(f32[32,1024]{1,0:T(8,128)S(1)} %get-tuple-element.4.res_in, f32[32,96]{1,0:T(8,128)S(1)} %get-tuple-element.5.res_out), custom_call_target="tpu_custom_call" | custom-call | tf_op jit(solution)/shard_map/pallas_call | solution.py:507
